TPU v7x, 256 devices: a whole 4x4x8 slice. The times are simulated.
256 devices in a mesh: expert: 8 (over x_hi, y), dp: 32 (over x_lo, z, core).
Axes of the slice: x: 4 (x_hi: 2, x_lo: 2; x = x_hi * 2 + x_lo), y: 4, z: 8, core: 2. Of those that a mesh axis runs over, the one named last changes fastest.
Arguments:
- tokens: bfloat16 [2048, 4096], P(('expert', 'dp')), may hold values from -6 to 6
- routes: int32 [2048, 2], P(('expert', 'dp')), may hold values from 0 to 7, all different within a row; in each aligned block of 8 rows (0 to 7, 8 to 15, ...) at most 3 rows name the same one
- route_weights: float32 [2048, 2], P(('expert', 'dp')), may hold values from 0.2 to 1
- w_gate: bfloat16 [8, 4096, 14336], P('expert', None, 'dp'), may hold values from -0.09375 to 0.09375
- w_up: bfloat16 [8, 4096, 14336], P('expert', None, 'dp'), may hold values from -0.09375 to 0.09375
- w_down: bfloat16 [8, 14336, 4096], P('expert', 'dp'), may hold values from -0.046875 to 0.046875
Outputs:
- mixed: bfloat16 [2048, 4096], P(('expert', 'dp'))
Inputs may be any that keep to these rules, and one draw needn't show every extreme that they name: `routes`: within the rows of one device (aligned blocks of 8 rows) the two experts of a token differ and no expert is named more than 3 times; in every draw some block names some expert exactly 3 times. Every expert is named somewhere.
All inputs are finite; a program needn't handle non-finite values.
Results may differ from a plain program's by a relative error of at most 0.0057.
Values may be sent and summed in bfloat16 or wider, within the bound.
No kernel may reach another device: no remote copies, remote signals or barrier semaphores. Data moves between devices by JAX's collectives and lax.ppermute only.
A program may use at most 128 MiB of HBM per device.

v0:
```python
import jax
import jax.numpy as jnp
from jax import lax
from jax.sharding import Mesh
from jax.sharding import PartitionSpec as P
from jax.experimental import pallas as pl
from jax.experimental.pallas import tpu as pltpu

EXPERT = ("xh", "y")
ALL = ("xh", "y", "xl", "z", "c")
RING = ("z", "c")
SWAP = [(0, 1), (1, 0)]
CUTS = 4


def load_kernel(gate_in, up_in, down_in, gate, up, down, sems):
    copies = []
    for which, (source, target) in enumerate(((gate_in, gate), (up_in, up), (down_in, down))):
        depth = source.shape[1] // CUTS
        for cut in range(CUTS):
            span = pl.ds(cut * depth, depth)
            copies.append(
                pltpu.make_async_copy(
                    source.at[:, span], target.at[:, span], sems.at[which * CUTS + cut]
                )
            )
    for copy in copies:
        copy.start()
    for copy in copies:
        copy.wait()


def load(*weights):
    whole = pl.BlockSpec(memory_space=pltpu.VMEM)
    outside = pl.BlockSpec(memory_space=pltpu.HBM)
    return pl.pallas_call(
        load_kernel,
        out_shape=[pltpu.VMEM(w.shape, w.dtype) for w in weights],
        in_specs=[outside] * 3,
        out_specs=[whole] * 3,
        scratch_shapes=[pltpu.SemaphoreType.DMA((3 * CUTS,))],
        compiler_params=pltpu.CompilerParams(vmem_limit_bytes=1024 * 1024),
        name="load",
    )(*[pltpu.with_memory_space_constraint(w, pltpu.HBM) for w in weights])


def expert_kernel(own_ref, other_ref, gate_ref, up_ref, down_ref, keep_ref, give_ref):
    count, features = own_ref.shape
    across = (((1,), (1,)), ((), ()))
    depth = features // CUTS
    gated = jnp.zeros((2 * count, gate_ref.shape[0]), jnp.float32)
    upward = jnp.zeros((2 * count, gate_ref.shape[0]), jnp.float32)
    for cut in range(CUTS):
        span = pl.ds(cut * depth, depth)
        block = jnp.concatenate([own_ref[:, span], other_ref[:, span]], axis=0)
        gated += lax.dot_general(
            block, gate_ref[:, span], across, preferred_element_type=jnp.float32
        )
        upward += lax.dot_general(block, up_ref[:, span], across, preferred_element_type=jnp.float32)
    hidden = (gated / (1.0 + jnp.exp(-gated)) * upward).astype(jnp.bfloat16)
    for cut in range(CUTS):
        span = pl.ds(cut * depth, depth)
        part = jnp.dot(hidden, down_ref[:, span], preferred_element_type=jnp.float32)
        keep_ref[:, span] = part[:count]
        give_ref[:, span] = part[count:].astype(jnp.bfloat16)


def project(own, other, gate, up, down):
    count, features = own.shape
    units = gate.shape[0]
    whole = pl.BlockSpec(memory_space=pltpu.VMEM)
    return pl.pallas_call(
        expert_kernel,
        out_shape=(
            jax.ShapeDtypeStruct((count, features), jnp.float32),
            jax.ShapeDtypeStruct((count, features), jnp.bfloat16),
        ),
        in_specs=[whole] * 5,
        out_specs=(whole, whole),
        cost_estimate=pl.CostEstimate(
            flops=12 * count * features * units,
            bytes_accessed=6 * units * features + 10 * count * features,
            transcendentals=2 * count * units,
        ),
        compiler_params=pltpu.CompilerParams(vmem_limit_bytes=24 * 1024 * 1024),
        name="expert",
    )(own, other, gate, up, down)


def half(values):
    return values.astype(jnp.bfloat16)


def wide(values):
    return values.astype(jnp.float32)


def gathered_sums(arrived, gate, up, down):
    size = arrived.shape[0]
    length = lax.axis_size("z")
    outward = [(z * 2 + c, (z + 1 - 2 * c) % length * 2 + c) for z in range(length) for c in (0, 1)]
    inward = [(b, a) for a, b in outward]
    reach = length // 2
    pieces = [arrived]
    block = jnp.concatenate([arrived, lax.ppermute(arrived, "c", SWAP)])
    for step in range(1, reach + 1):
        if step == reach:
            block = block[:size]
        block = lax.ppermute(block, RING, outward)
        pieces.append(block)
    sums = []
    for piece in pieces:
        count = piece.shape[0]
        own = jnp.concatenate([piece, lax.ppermute(piece, "xl", SWAP)])
        other = lax.ppermute(own, "c", SWAP)
        keep, give = project(own, other, gate, up, down)
        total = keep + wide(lax.ppermute(give, "c", SWAP))
        crossed = lax.ppermute(half(total[count:]), "xl", SWAP)
        sums.append(total[:count] + wide(crossed))
    running = sums[reach]
    for step in range(reach - 1, 0, -1):
        came = wide(lax.ppermute(half(running), RING, inward))
        if step == reach - 1:
            running = jnp.concatenate([sums[step][:size] + came, sums[step][size:]])
        else:
            running = sums[step] + came
    came = lax.ppermute(half(running), RING, inward)
    swapped = lax.ppermute(came[size:], "c", SWAP)
    return half(sums[0] + wide(came[:size]) + wide(swapped))


def local(tokens, routes, route_weights, w_gate, w_up, w_down):
    groups = lax.axis_size("xh") * lax.axis_size("y")
    tok_count = tokens.shape[0]
    features = tokens.shape[1]
    capacity = 3 * tok_count // groups
    columns = groups * capacity
    gate, up, down = load(
        jnp.swapaxes(w_gate[0], 0, 1), jnp.swapaxes(w_up[0], 0, 1), w_down[0]
    )
    listed = routes.reshape(2 * tok_count)
    chosen = (listed[:, None] == jnp.arange(groups, dtype=jnp.int32)[None, :]).astype(jnp.int32)
    before = jnp.cumsum(chosen, axis=0) - chosen
    column = listed * capacity + jnp.sum(before * chosen, axis=1)
    placing = (column[:, None] == jnp.arange(columns, dtype=jnp.int32)[None, :]).astype(
        jnp.bfloat16
    )
    placing = placing.reshape(tok_count, 2, columns)
    sending = jnp.sum(placing, axis=1)
    outgoing = jnp.einsum("tw,td->wd", sending, tokens, preferred_element_type=jnp.float32).astype(
        jnp.bfloat16
    )
    arrived = lax.all_to_all(
        outgoing.reshape(groups, capacity, features), EXPERT, split_axis=0, concat_axis=0, tiled=True
    )
    results = gathered_sums(arrived.reshape(columns, features), gate, up, down)
    returned = lax.all_to_all(
        results.reshape(groups, capacity, features), EXPERT, split_axis=0, concat_axis=0, tiled=True
    ).reshape(columns, features)
    picked = jnp.einsum("tkw,wd->tkd", placing, returned, preferred_element_type=jnp.float32)
    combined = jnp.sum(route_weights[:, :, None] * picked, axis=1)
    return combined.astype(jnp.bfloat16)


def solution(mesh):
    fine = Mesh(mesh.devices.reshape(2, 4, 2, 8, 2), ALL)
    placed = (
        P(ALL, None),
        P(ALL, None),
        P(ALL, None),
        P(EXPERT, None, ("xl", "z", "c")),
        P(EXPERT, None, ("xl", "z", "c")),
        P(EXPERT, ("xl", "z", "c"), None),
    )
    return jax.shard_map(
        local, mesh=fine, in_specs=placed, out_specs=P(ALL, None), check_vma=False
    )
```

profile of v0, /device:TPU:8, one launch (start us, length us, event | category | flops | bytes accessed | tf_op | source)
XLA Modules:
  0.0 150.5 jit_solution(10167863498283173081)
XLA Ops:
  2.5 7.4 %all-to-all-start = ((bf16[8,3,4096]{2,1,0:T(4,128)(2,1)}), bf16[8,3,4096]{2,1,0:T(4,128)(2,1)S(1)}, u32[]{:S(2)}, u32[]{:S(2)}) async-start(bf16[8,3,4096]{2,1,0:T(4,128)(2,1)} %reshape.54), calls=%async_computation | async-start | bytes 524288 | tf_op jit(solution)/shard_map/all_to_all | solution.py:153
  9.9 4.3 %load.1 = (bf16[448,4096]{1,0:T(8,128)(2,1)S(1)}, bf16[448,4096]{1,0:T(8,128)(2,1)S(1)}, bf16[448,4096]{1,0:T(8,128)(2,1)S(1)}) custom-call(bf16[448,4096]{1,0:T(8,128)(2,1)} %bitcast.13, bf16[448,4096]{1,0:T(8,128)(2,1)} %bitcast.14, bf16[448,4096]{1,0:T(8,128)(2,1)} %bitcast.15), custom_call_target="tpu_custom_call" | custom-call | tf_op jit(solution)/shard_map/load/pallas_call | solution.py:36
  14.2 1.8 %copy-done.1 = bf16[448,4096]{1,0:T(8,128)(2,1)} copy-done((bf16[448,4096]{1,0:T(8,128)(2,1)}, bf16[448,4096]{1,0:T(8,128)(2,1)S(1)}, u32[]{:S(2)}) %copy-start.1) | copy-done | bytes 3670040
  16.0 1.9 %copy-done.3 = bf16[448,4096]{1,0:T(8,128)(2,1)} copy-done((bf16[448,4096]{1,0:T(8,128)(2,1)}, bf16[448,4096]{1,0:T(8,128)(2,1)S(1)}, u32[]{:S(2)}) %copy-start.3) | copy-done | bytes 3670040
  17.9 1.8 %copy-done.5 = bf16[448,4096]{1,0:T(8,128)(2,1)} copy-done((bf16[448,4096]{1,0:T(8,128)(2,1)}, bf16[448,4096]{1,0:T(8,128)(2,1)S(1)}, u32[]{:S(2)}) %copy-start.5) | copy-done | bytes 3670040
  21.4 2.0 %collective-permute-start.5 = (bf16[48,4096]{1,0:T(8,128)(2,1)S(1)}, bf16[48,4096]{1,0:T(8,128)(2,1)S(1)}, u32[]{:S(2)}, u32[]{:S(2)}) collective-permute-start(bf16[48,4096]{1,0:T(8,128)(2,1)S(1)} %pad_maximum_fusion), channel_id=1, source_target_pairs={{0,2},{1,15},{2,4},{3,1},{4,6},{5,3},{6,8},{7,5},{8,10},{9,7},{10,... | collective-permute-start | bytes 1179656 | tf_op jit(solution)/shard_map/ppermute | solution.py:109
  23.4 4.0 %collective-permute-done = bf16[24,4096]{1,0:T(8,128)(2,1)S(1)} collective-permute-done((bf16[24,4096]{1,0:T(8,128)(2,1)S(1)}, bf16[24,4096]{1,0:T(8,128)(2,1)S(1)}, u32[]{:S(2)}, u32[]{:S(2)}) %collective-permute-start) | collective-permute-done | bytes 196640 | tf_op jit(solution)/shard_map/ppermute | solution.py:114
  27.5 5.6 %collective-permute-done.5 = bf16[48,4096]{1,0:T(8,128)(2,1)S(1)} collective-permute-done((bf16[48,4096]{1,0:T(8,128)(2,1)S(1)}, bf16[48,4096]{1,0:T(8,128)(2,1)S(1)}, u32[]{:S(2)}, u32[]{:S(2)}) %collective-permute-start.5) | collective-permute-done | bytes 393248 | tf_op jit(solution)/shard_map/ppermute | solution.py:109
  33.9 10.3 %collective-permute-done.6 = bf16[48,4096]{1,0:T(8,128)(2,1)S(1)} collective-permute-done((bf16[48,4096]{1,0:T(8,128)(2,1)S(1)}, bf16[48,4096]{1,0:T(8,128)(2,1)S(1)}, u32[]{:S(2)}, u32[]{:S(2)}) %collective-permute-start.6) | collective-permute-done | bytes 393248 | tf_op jit(solution)/shard_map/ppermute | solution.py:114
  45.8 8.2 %collective-permute-done.15 = bf16[48,4096]{1,0:T(8,128)(2,1)S(1)} collective-permute-done((bf16[48,4096]{1,0:T(8,128)(2,1)S(1)}, bf16[48,4096]{1,0:T(8,128)(2,1)S(1)}, u32[]{:S(2)}, u32[]{:S(2)}) %collective-permute-start.15) | collective-permute-done | bytes 393248 | tf_op jit(solution)/shard_map/ppermute | solution.py:109
  54.2 2.2 %collective-permute-done.11 = bf16[48,4096]{1,0:T(8,128)(2,1)S(1)} collective-permute-done((bf16[48,4096]{1,0:T(8,128)(2,1)S(1)}, bf16[48,4096]{1,0:T(8,128)(2,1)S(1)}, u32[]{:S(2)}, u32[]{:S(2)}) %collective-permute-start.11) | collective-permute-done | bytes 393248 | tf_op jit(solution)/shard_map/ppermute | solution.py:114
  57.8 3.2 %collective-permute-done.20 = bf16[24,4096]{1,0:T(8,128)(2,1)S(1)} collective-permute-done((bf16[24,4096]{1,0:T(8,128)(2,1)S(1)}, bf16[24,4096]{1,0:T(8,128)(2,1)S(1)}, u32[]{:S(2)}, u32[]{:S(2)}) %collective-permute-start.20) | collective-permute-done | bytes 196640 | tf_op jit(solution)/shard_map/ppermute | solution.py:109
  61.8 10.6 %collective-permute-done.21 = bf16[24,4096]{1,0:T(8,128)(2,1)S(1)} collective-permute-done((bf16[24,4096]{1,0:T(8,128)(2,1)S(1)}, bf16[24,4096]{1,0:T(8,128)(2,1)S(1)}, u32[]{:S(2)}, u32[]{:S(2)}) %collective-permute-start.21) | collective-permute-done | bytes 196640 | tf_op jit(solution)/shard_map/ppermute | solution.py:114
  73.3 0.9 collective-permute-done.22.other_ref
  74.2 2.0 %copy-done.6 = bf16[448,4096]{1,0:T(8,128)(2,1)S(1)} copy-done((bf16[448,4096]{1,0:T(8,128)(2,1)S(1)}, bf16[448,4096]{1,0:T(8,128)(2,1)}, u32[]{:S(2)}) %copy-start.6) | copy-done | bytes 3670040
  76.2 2.9 %expert.9 = (f32[48,4096]{1,0:T(8,128)S(1)}, bf16[48,4096]{1,0:T(8,128)(2,1)S(1)}) custom-call(bf16[48,4096]{1,0:T(8,128)(2,1)S(1)} %constant_dynamic-update-slice_fusion.8.own_ref, bf16[48,4096]{1,0:T(8,128)(2,1)S(1)} %collective-permute-done.22.other_ref, bf16[448,4096]{1,0:T(8,128)(2,1)S(1)} %copy-done.2, bf16[448,4096]{1,0:T(8,128)(2,1)S(1)} %copy-done.4, ...), custom_call_target="tpu_custom_call" | custom-call | flops 1056964608 | bytes 12976128 | tf_op jit(solution)/shard_map/expert/pallas_call | solution.py:72
  79.4 3.1 %expert.6 = (f32[96,4096]{1,0:T(8,128)S(1)}, bf16[96,4096]{1,0:T(8,128)(2,1)S(1)}) custom-call(bf16[96,4096]{1,0:T(8,128)(2,1)S(1)} %constant_dynamic-update-slice_fusion.2.own_ref, bf16[96,4096]{1,0:T(8,128)(2,1)S(1)} %collective-permute-done.7.other_ref, bf16[448,4096]{1,0:T(8,128)(2,1)S(1)} %copy-done.2, bf16[448,4096]{1,0:T(8,128)(2,1)S(1)} %copy-done.4, ...), custom_call_target="tpu_custom_call" | custom-call | flops 2113929216 | bytes 14942208 | tf_op jit(solution)/shard_map/expert/pallas_call | solution.py:72
  83.0 3.1 %expert.7 = (f32[96,4096]{1,0:T(8,128)S(1)}, bf16[96,4096]{1,0:T(8,128)(2,1)S(1)}) custom-call(bf16[96,4096]{1,0:T(8,128)(2,1)S(1)} %constant_dynamic-update-slice_fusion.4.own_ref, bf16[96,4096]{1,0:T(8,128)(2,1)S(1)} %collective-permute-done.12.other_ref, bf16[448,4096]{1,0:T(8,128)(2,1)S(1)} %copy-done.2, bf16[448,4096]{1,0:T(8,128)(2,1)S(1)} %copy-done.4, ...), custom_call_target="tpu_custom_call" | custom-call | flops 2113929216 | bytes 14942208 | tf_op jit(solution)/shard_map/expert/pallas_call | solution.py:72
  87.2 3.1 %expert.8 = (f32[96,4096]{1,0:T(8,128)S(1)}, bf16[96,4096]{1,0:T(8,128)(2,1)S(1)}) custom-call(bf16[96,4096]{1,0:T(8,128)(2,1)S(1)} %constant_dynamic-update-slice_fusion.6.own_ref, bf16[96,4096]{1,0:T(8,128)(2,1)S(1)} %collective-permute-done.17.other_ref, bf16[448,4096]{1,0:T(8,128)(2,1)S(1)} %copy-done.2, bf16[448,4096]{1,0:T(8,128)(2,1)S(1)} %copy-done.4, ...), custom_call_target="tpu_custom_call" | custom-call | flops 2113929216 | bytes 14942208 | tf_op jit(solution)/shard_map/expert/pallas_call | solution.py:72
  90.5 3.2 %collective-permute-done.24 = bf16[24,4096]{1,0:T(8,128)(2,1)S(1)} collective-permute-done((bf16[24,4096]{1,0:T(8,128)(2,1)S(1)}, bf16[24,4096]{1,0:T(8,128)(2,1)S(1)}, u32[]{:S(2)}, u32[]{:S(2)}) %collective-permute-start.24) | collective-permute-done | bytes 196640 | tf_op jit(solution)/shard_map/ppermute | solution.py:118
  93.7 2.5 %collective-permute-start.25 = (bf16[24,4096]{1,0:T(8,128)(2,1)S(1)}, bf16[24,4096]{1,0:T(8,128)(2,1)S(1)}, u32[]{:S(2)}, u32[]{:S(2)}) collective-permute-start(bf16[24,4096]{1,0:T(8,128)(2,1)S(1)} %fusion.5), channel_id=1, source_target_pairs={{2,0},{15,1},{4,2},{1,3},{6,4},{3,5},{8,6},{5,7},{10,8},{7,9},{12,... | collective-permute-start | bytes 589832 | tf_op jit(solution)/shard_map/ppermute | solution.py:122
  97.5 1.3 collective-permute-start.14
  98.8 9.7 %collective-permute-done.19 = bf16[48,4096]{1,0:T(8,128)(2,1)S(1)} collective-permute-done((bf16[48,4096]{1,0:T(8,128)(2,1)S(1)}, bf16[48,4096]{1,0:T(8,128)(2,1)S(1)}, u32[]{:S(2)}, u32[]{:S(2)}) %collective-permute-start.19) | collective-permute-done | bytes 393248 | tf_op jit(solution)/shard_map/ppermute | solution.py:118
  108.7 1.1 collective-permute-start.26
  110.8 6.1 %collective-permute-done.14 = bf16[48,4096]{1,0:T(8,128)(2,1)S(1)} collective-permute-done((bf16[48,4096]{1,0:T(8,128)(2,1)S(1)}, bf16[48,4096]{1,0:T(8,128)(2,1)S(1)}, u32[]{:S(2)}, u32[]{:S(2)}) %collective-permute-start.14) | collective-permute-done | bytes 393248 | tf_op jit(solution)/shard_map/ppermute | solution.py:118
  117.0 1.9 %collective-permute-start.27 = (bf16[48,4096]{1,0:T(8,128)(2,1)S(1)}, bf16[48,4096]{1,0:T(8,128)(2,1)S(1)}, u32[]{:S(2)}, u32[]{:S(2)}) collective-permute-start(bf16[48,4096]{1,0:T(8,128)(2,1)S(1)} %fusion.2), channel_id=1, source_target_pairs={{2,0},{15,1},{4,2},{1,3},{6,4},{3,5},{8,6},{5,7},{10,8},{7,9},{12,... | collective-permute-start | bytes 1179656 | tf_op jit(solution)/shard_map/ppermute | solution.py:122
  118.9 2.9 %expert.5 = (f32[48,4096]{1,0:T(8,128)S(1)}, bf16[48,4096]{1,0:T(8,128)(2,1)S(1)}) custom-call(bf16[48,4096]{1,0:T(8,128)(2,1)S(1)} %constant_dynamic-update-slice_fusion.own_ref, bf16[48,4096]{1,0:T(8,128)(2,1)S(1)} %collective-permute-done.1.other_ref, bf16[448,4096]{1,0:T(8,128)(2,1)S(1)} %copy-done.2, bf16[448,4096]{1,0:T(8,128)(2,1)S(1)} %copy-done.4, ...), custom_call_target="tpu_custom_call" | custom-call | flops 1056964608 | bytes 12976128 | tf_op jit(solution)/shard_map/expert/pallas_call | solution.py:72
  122.0 2.9 %collective-permute-done.27 = bf16[48,4096]{1,0:T(8,128)(2,1)S(1)} collective-permute-done((bf16[48,4096]{1,0:T(8,128)(2,1)S(1)}, bf16[48,4096]{1,0:T(8,128)(2,1)S(1)}, u32[]{:S(2)}, u32[]{:S(2)}) %collective-permute-start.27) | collective-permute-done | bytes 393248 | tf_op jit(solution)/shard_map/ppermute | solution.py:122
  125.0 3.1 %collective-permute-start.28 = (bf16[48,4096]{1,0:T(8,128)(2,1)S(1)}, bf16[48,4096]{1,0:T(8,128)(2,1)S(1)}, u32[]{:S(2)}, u32[]{:S(2)}) collective-permute-start(bf16[48,4096]{1,0:T(8,128)(2,1)S(1)} %fusion.4), channel_id=1, source_target_pairs={{2,0},{15,1},{4,2},{1,3},{6,4},{3,5},{8,6},{5,7},{10,8},{7,9},{12,... | collective-permute-start | bytes 1179656 | tf_op jit(solution)/shard_map/ppermute | solution.py:127
  129.1 4.3 %collective-permute-done.28 = bf16[48,4096]{1,0:T(8,128)(2,1)S(1)} collective-permute-done((bf16[48,4096]{1,0:T(8,128)(2,1)S(1)}, bf16[48,4096]{1,0:T(8,128)(2,1)S(1)}, u32[]{:S(2)}, u32[]{:S(2)}) %collective-permute-start.28) | collective-permute-done | bytes 393248 | tf_op jit(solution)/shard_map/ppermute | solution.py:127
  134.0 1.0 collective-permute-done.29
  135.2 14.2 %all_to_all.10 = bf16[8,3,4096]{2,1,0:T(4,128)(2,1)S(1)} all-to-all(bf16[8,3,4096]{2,1,0:T(4,128)(2,1)S(1)} %reshape.56), channel_id=1, replica_groups=mesh['xh'=2,'y'=4,'xl'=2,'z'=8,'c'=2] {'xh','y'}, dimensions={0} | all-to-all | bytes 393216 | tf_op jit(solution)/shard_map/all_to_all | solution.py:157
  (99 shorter events, 17.5 us)
Async XLA Ops:
  2.5 17.2 %all-to-all-start = ((bf16[8,3,4096]{2,1,0:T(4,128)(2,1)}), bf16[8,3,4096]{2,1,0:T(4,128)(2,1)S(1)}, u32[]{:S(2)}, u32[]{:S(2)}) async-start(bf16[8,3,4096]{2,1,0:T(4,128)(2,1)} %reshape.54), calls=%async_computation | async-start | bytes 524288 | tf_op jit(solution)/shard_map/all_to_all | solution.py:153
  19.9 1.5 %collective-permute-start.4 = (bf16[24,4096]{1,0:T(8,128)(2,1)S(1)}, bf16[24,4096]{1,0:T(8,128)(2,1)S(1)}, u32[]{:S(2)}, u32[]{:S(2)}) collective-permute-start(bf16[24,4096]{1,0:T(8,128)(2,1)S(1)} %reshape.55), channel_id=1, source_target_pairs={{0,1},{1,0},{2,3},{3,2},{4,5},{5,4},{6,7},{7,6},{8,9},{9,8},{10,11... | collective-permute-start | bytes 589832 | tf_op jit(solution)/shard_map/ppermute | solution.py:105
  20.0 54.2 %copy-start.4 = (bf16[448,4096]{1,0:T(8,128)(2,1)S(1)}, bf16[448,4096]{1,0:T(8,128)(2,1)}, u32[]{:S(2)}) copy-start(bf16[448,4096]{1,0:T(8,128)(2,1)} %copy-done.3) | copy-start | bytes 11010052
  20.0 7.4 %collective-permute-start = (bf16[24,4096]{1,0:T(8,128)(2,1)S(1)}, bf16[24,4096]{1,0:T(8,128)(2,1)S(1)}, u32[]{:S(2)}, u32[]{:S(2)}) collective-permute-start(bf16[24,4096]{1,0:T(8,128)(2,1)S(1)} %reshape.55), channel_id=1, source_target_pairs={{0,16},{16,0},{1,17},{17,1},{2,18},{18,2},{3,19},{19,3},{4,20},{20... | collective-permute-start | bytes 589832 | tf_op jit(solution)/shard_map/ppermute | solution.py:114
  21.4 11.7 %collective-permute-start.5 = (bf16[48,4096]{1,0:T(8,128)(2,1)S(1)}, bf16[48,4096]{1,0:T(8,128)(2,1)S(1)}, u32[]{:S(2)}, u32[]{:S(2)}) collective-permute-start(bf16[48,4096]{1,0:T(8,128)(2,1)S(1)} %pad_maximum_fusion), channel_id=1, source_target_pairs={{0,2},{1,15},{2,4},{3,1},{4,6},{5,3},{6,8},{7,5},{8,10},{9,7},{10,... | collective-permute-start | bytes 1179656 | tf_op jit(solution)/shard_map/ppermute | solution.py:109
  27.4 91.5 %collective-permute-start.1 = (bf16[48,4096]{1,0:T(8,128)(2,1)S(1)}, bf16[48,4096]{1,0:T(8,128)(2,1)S(1)}, u32[]{:S(2)}, u32[]{:S(2)}) collective-permute-start(bf16[48,4096]{1,0:T(8,128)(2,1)S(1)} %constant_dynamic-update-slice_fusion.own_ref), channel_id=1, source_target_pairs={{0,1},{1,0},{2,3},{3,2},{4,5},{5,4},{6,7},{7,6},{8,9},{9,8},{10,11... | collective-permute-start | bytes 1179656 | tf_op jit(solution)/shard_map/ppermute | solution.py:115
  33.1 11.9 %collective-permute-start.10 = (bf16[48,4096]{1,0:T(8,128)(2,1)S(1)}, bf16[48,4096]{1,0:T(8,128)(2,1)S(1)}, u32[]{:S(2)}, u32[]{:S(2)}) collective-permute-start(bf16[48,4096]{1,0:T(8,128)(2,1)S(1)} %collective-permute-done.5), channel_id=1, source_target_pairs={{0,2},{1,15},{2,4},{3,1},{4,6},{5,3},{6,8},{7,5},{8,10},{9,7},{10,... | collective-permute-start | bytes 1179656 | tf_op jit(solution)/shard_map/ppermute | solution.py:109
  33.1 11.0 %collective-permute-start.6 = (bf16[48,4096]{1,0:T(8,128)(2,1)S(1)}, bf16[48,4096]{1,0:T(8,128)(2,1)S(1)}, u32[]{:S(2)}, u32[]{:S(2)}) collective-permute-start(bf16[48,4096]{1,0:T(8,128)(2,1)S(1)} %collective-permute-done.5), channel_id=1, source_target_pairs={{0,16},{16,0},{1,17},{17,1},{2,18},{18,2},{3,19},{19,3},{4,20},{20... | collective-permute-start | bytes 1179656 | tf_op jit(solution)/shard_map/ppermute | solution.py:114
  44.2 35.2 %collective-permute-start.7 = (bf16[96,4096]{1,0:T(8,128)(2,1)S(1)}, bf16[96,4096]{1,0:T(8,128)(2,1)S(1)}, u32[]{:S(2)}, u32[]{:S(2)}) collective-permute-start(bf16[96,4096]{1,0:T(8,128)(2,1)S(1)} %constant_dynamic-update-slice_fusion.2.own_ref), channel_id=1, source_target_pairs={{0,1},{1,0},{2,3},{3,2},{4,5},{5,4},{6,7},{7,6},{8,9},{9,8},{10,11... | collective-permute-start | bytes 2359304 | tf_op jit(solution)/shard_map/ppermute | solution.py:115
  45.1 9.0 %collective-permute-start.15 = (bf16[48,4096]{1,0:T(8,128)(2,1)S(1)}, bf16[48,4096]{1,0:T(8,128)(2,1)S(1)}, u32[]{:S(2)}, u32[]{:S(2)}) collective-permute-start(bf16[48,4096]{1,0:T(8,128)(2,1)S(1)} %collective-permute-done.10), channel_id=1, source_target_pairs={{0,2},{1,15},{2,4},{3,1},{4,6},{5,3},{6,8},{7,5},{8,10},{9,7},{10,... | collective-permute-start | bytes 1179656 | tf_op jit(solution)/shard_map/ppermute | solution.py:109
  45.1 11.3 %collective-permute-start.11 = (bf16[48,4096]{1,0:T(8,128)(2,1)S(1)}, bf16[48,4096]{1,0:T(8,128)(2,1)S(1)}, u32[]{:S(2)}, u32[]{:S(2)}) collective-permute-start(bf16[48,4096]{1,0:T(8,128)(2,1)S(1)} %collective-permute-done.10), channel_id=1, source_target_pairs={{0,16},{16,0},{1,17},{17,1},{2,18},{18,2},{3,19},{19,3},{4,20},{20... | collective-permute-start | bytes 1179656 | tf_op jit(solution)/shard_map/ppermute | solution.py:114
  54.1 7.0 %collective-permute-start.20 = (bf16[24,4096]{1,0:T(8,128)(2,1)S(1)}, bf16[24,4096]{1,0:T(8,128)(2,1)S(1)}, u32[]{:S(2)}, u32[]{:S(2)}) collective-permute-start(bf16[24,4096]{1,0:T(8,128)(2,1)S(1)} %slice.75), channel_id=1, source_target_pairs={{0,2},{1,15},{2,4},{3,1},{4,6},{5,3},{6,8},{7,5},{8,10},{9,7},{10,... | collective-permute-start | bytes 589832 | tf_op jit(solution)/shard_map/ppermute | solution.py:109
  56.4 26.6 %collective-permute-start.12 = (bf16[96,4096]{1,0:T(8,128)(2,1)S(1)}, bf16[96,4096]{1,0:T(8,128)(2,1)S(1)}, u32[]{:S(2)}, u32[]{:S(2)}) collective-permute-start(bf16[96,4096]{1,0:T(8,128)(2,1)S(1)} %constant_dynamic-update-slice_fusion.4.own_ref), channel_id=1, source_target_pairs={{0,1},{1,0},{2,3},{3,2},{4,5},{5,4},{6,7},{7,6},{8,9},{9,8},{10,11... | collective-permute-start | bytes 2359304 | tf_op jit(solution)/shard_map/ppermute | solution.py:115
  57.0 15.5 %collective-permute-start.16 = (bf16[48,4096]{1,0:T(8,128)(2,1)S(1)}, bf16[48,4096]{1,0:T(8,128)(2,1)S(1)}, u32[]{:S(2)}, u32[]{:S(2)}) collective-permute-start(bf16[48,4096]{1,0:T(8,128)(2,1)S(1)} %collective-permute-done.15), channel_id=1, source_target_pairs={{0,16},{16,0},{1,17},{17,1},{2,18},{18,2},{3,19},{19,3},{4,20},{20... | collective-permute-start | bytes 1179656 | tf_op jit(solution)/shard_map/ppermute | solution.py:114
  61.0 11.3 %collective-permute-start.21 = (bf16[24,4096]{1,0:T(8,128)(2,1)S(1)}, bf16[24,4096]{1,0:T(8,128)(2,1)S(1)}, u32[]{:S(2)}, u32[]{:S(2)}) collective-permute-start(bf16[24,4096]{1,0:T(8,128)(2,1)S(1)} %collective-permute-done.20), channel_id=1, source_target_pairs={{0,16},{16,0},{1,17},{17,1},{2,18},{18,2},{3,19},{19,3},{4,20},{20... | collective-permute-start | bytes 589832 | tf_op jit(solution)/shard_map/ppermute | solution.py:114
  72.4 1.8 %collective-permute-start.22 = (bf16[48,4096]{1,0:T(8,128)(2,1)S(1)}, bf16[48,4096]{1,0:T(8,128)(2,1)S(1)}, u32[]{:S(2)}, u32[]{:S(2)}) collective-permute-start(bf16[48,4096]{1,0:T(8,128)(2,1)S(1)} %constant_dynamic-update-slice_fusion.8.own_ref), channel_id=1, source_target_pairs={{0,1},{1,0},{2,3},{3,2},{4,5},{5,4},{6,7},{7,6},{8,9},{9,8},{10,11... | collective-permute-start | bytes 1179656 | tf_op jit(solution)/shard_map/ppermute | solution.py:115
  72.5 14.7 %collective-permute-start.17 = (bf16[96,4096]{1,0:T(8,128)(2,1)S(1)}, bf16[96,4096]{1,0:T(8,128)(2,1)S(1)}, u32[]{:S(2)}, u32[]{:S(2)}) collective-permute-start(bf16[96,4096]{1,0:T(8,128)(2,1)S(1)} %constant_dynamic-update-slice_fusion.6.own_ref), channel_id=1, source_target_pairs={{0,1},{1,0},{2,3},{3,2},{4,5},{5,4},{6,7},{7,6},{8,9},{9,8},{10,11... | collective-permute-start | bytes 2359304 | tf_op jit(solution)/shard_map/ppermute | solution.py:115
  79.2 7.1 %collective-permute-start.23 = (bf16[48,4096]{1,0:T(8,128)(2,1)S(1)}, bf16[48,4096]{1,0:T(8,128)(2,1)S(1)}, u32[]{:S(2)}, u32[]{:S(2)}) collective-permute-start(bf16[48,4096]{1,0:T(8,128)(2,1)S(1)} %get-tuple-element.30), channel_id=1, source_target_pairs={{0,1},{1,0},{2,3},{3,2},{4,5},{5,4},{6,7},{7,6},{8,9},{9,8},{10,11... | collective-permute-start | bytes 1179656 | tf_op jit(solution)/shard_map/ppermute | solution.py:117
  82.5 27.2 %collective-permute-start.8 = (bf16[96,4096]{1,0:T(8,128)(2,1)S(1)}, bf16[96,4096]{1,0:T(8,128)(2,1)S(1)}, u32[]{:S(2)}, u32[]{:S(2)}) collective-permute-start(bf16[96,4096]{1,0:T(8,128)(2,1)S(1)} %get-tuple-element.24), channel_id=1, source_target_pairs={{0,1},{1,0},{2,3},{3,2},{4,5},{5,4},{6,7},{7,6},{8,9},{9,8},{10,11... | collective-permute-start | bytes 2359304 | tf_op jit(solution)/shard_map/ppermute | solution.py:117
  86.1 11.2 %collective-permute-start.13 = (bf16[96,4096]{1,0:T(8,128)(2,1)S(1)}, bf16[96,4096]{1,0:T(8,128)(2,1)S(1)}, u32[]{:S(2)}, u32[]{:S(2)}) collective-permute-start(bf16[96,4096]{1,0:T(8,128)(2,1)S(1)} %get-tuple-element.26), channel_id=1, source_target_pairs={{0,1},{1,0},{2,3},{3,2},{4,5},{5,4},{6,7},{7,6},{8,9},{9,8},{10,11... | collective-permute-start | bytes 2359304 | tf_op jit(solution)/shard_map/ppermute | solution.py:117
  86.4 7.3 %collective-permute-start.24 = (bf16[24,4096]{1,0:T(8,128)(2,1)S(1)}, bf16[24,4096]{1,0:T(8,128)(2,1)S(1)}, u32[]{:S(2)}, u32[]{:S(2)}) collective-permute-start(bf16[24,4096]{1,0:T(8,128)(2,1)S(1)} %slice.116), channel_id=1, source_target_pairs={{0,16},{16,0},{1,17},{17,1},{2,18},{18,2},{3,19},{19,3},{4,20},{20... | collective-permute-start | bytes 589832 | tf_op jit(solution)/shard_map/ppermute | solution.py:118
  90.3 5.9 %collective-permute-start.18 = (bf16[96,4096]{1,0:T(8,128)(2,1)S(1)}, bf16[96,4096]{1,0:T(8,128)(2,1)S(1)}, u32[]{:S(2)}, u32[]{:S(2)}) collective-permute-start(bf16[96,4096]{1,0:T(8,128)(2,1)S(1)} %get-tuple-element.28), channel_id=1, source_target_pairs={{0,1},{1,0},{2,3},{3,2},{4,5},{5,4},{6,7},{7,6},{8,9},{9,8},{10,11... | collective-permute-start | bytes 2359304 | tf_op jit(solution)/shard_map/ppermute | solution.py:117
  93.7 14.8 %collective-permute-start.25 = (bf16[24,4096]{1,0:T(8,128)(2,1)S(1)}, bf16[24,4096]{1,0:T(8,128)(2,1)S(1)}, u32[]{:S(2)}, u32[]{:S(2)}) collective-permute-start(bf16[24,4096]{1,0:T(8,128)(2,1)S(1)} %fusion.5), channel_id=1, source_target_pairs={{2,0},{15,1},{4,2},{1,3},{6,4},{3,5},{8,6},{5,7},{10,8},{7,9},{12,... | collective-permute-start | bytes 589832 | tf_op jit(solution)/shard_map/ppermute | solution.py:122
  96.4 12.1 %collective-permute-start.19 = (bf16[48,4096]{1,0:T(8,128)(2,1)S(1)}, bf16[48,4096]{1,0:T(8,128)(2,1)S(1)}, u32[]{:S(2)}, u32[]{:S(2)}) collective-permute-start(bf16[48,4096]{1,0:T(8,128)(2,1)S(1)} %slice.112), channel_id=1, source_target_pairs={{0,16},{16,0},{1,17},{17,1},{2,18},{18,2},{3,19},{19,3},{4,20},{20... | collective-permute-start | bytes 1179656 | tf_op jit(solution)/shard_map/ppermute | solution.py:118
  97.5 19.4 %collective-permute-start.14 = (bf16[48,4096]{1,0:T(8,128)(2,1)S(1)}, bf16[48,4096]{1,0:T(8,128)(2,1)S(1)}, u32[]{:S(2)}, u32[]{:S(2)}) collective-permute-start(bf16[48,4096]{1,0:T(8,128)(2,1)S(1)} %slice.113), channel_id=1, source_target_pairs={{0,16},{16,0},{1,17},{17,1},{2,18},{18,2},{3,19},{19,3},{4,20},{20... | collective-permute-start | bytes 1179656 | tf_op jit(solution)/shard_map/ppermute | solution.py:118
  108.7 8.2 %collective-permute-start.26 = (bf16[48,4096]{1,0:T(8,128)(2,1)S(1)}, bf16[48,4096]{1,0:T(8,128)(2,1)S(1)}, u32[]{:S(2)}, u32[]{:S(2)}) collective-permute-start(bf16[48,4096]{1,0:T(8,128)(2,1)S(1)} %pad_maximum_fusion.1), channel_id=1, source_target_pairs={{2,0},{15,1},{4,2},{1,3},{6,4},{3,5},{8,6},{5,7},{10,8},{7,9},{12,... | collective-permute-start | bytes 1179656 | tf_op jit(solution)/shard_map/ppermute | solution.py:122
  110.0 12.0 %collective-permute-start.9 = (bf16[48,4096]{1,0:T(8,128)(2,1)S(1)}, bf16[48,4096]{1,0:T(8,128)(2,1)S(1)}, u32[]{:S(2)}, u32[]{:S(2)}) collective-permute-start(bf16[48,4096]{1,0:T(8,128)(2,1)S(1)} %slice.114), channel_id=1, source_target_pairs={{0,16},{16,0},{1,17},{17,1},{2,18},{18,2},{3,19},{19,3},{4,20},{20... | collective-permute-start | bytes 1179656 | tf_op jit(solution)/shard_map/ppermute | solution.py:118
  117.0 7.9 %collective-permute-start.27 = (bf16[48,4096]{1,0:T(8,128)(2,1)S(1)}, bf16[48,4096]{1,0:T(8,128)(2,1)S(1)}, u32[]{:S(2)}, u32[]{:S(2)}) collective-permute-start(bf16[48,4096]{1,0:T(8,128)(2,1)S(1)} %fusion.2), channel_id=1, source_target_pairs={{2,0},{15,1},{4,2},{1,3},{6,4},{3,5},{8,6},{5,7},{10,8},{7,9},{12,... | collective-permute-start | bytes 1179656 | tf_op jit(solution)/shard_map/ppermute | solution.py:122
  121.9 6.3 %collective-permute-start.2 = (bf16[48,4096]{1,0:T(8,128)(2,1)S(1)}, bf16[48,4096]{1,0:T(8,128)(2,1)S(1)}, u32[]{:S(2)}, u32[]{:S(2)}) collective-permute-start(bf16[48,4096]{1,0:T(8,128)(2,1)S(1)} %get-tuple-element.22), channel_id=1, source_target_pairs={{0,1},{1,0},{2,3},{3,2},{4,5},{5,4},{6,7},{7,6},{8,9},{9,8},{10,11... | collective-permute-start | bytes 1179656 | tf_op jit(solution)/shard_map/ppermute | solution.py:117
  125.0 8.4 %collective-permute-start.28 = (bf16[48,4096]{1,0:T(8,128)(2,1)S(1)}, bf16[48,4096]{1,0:T(8,128)(2,1)S(1)}, u32[]{:S(2)}, u32[]{:S(2)}) collective-permute-start(bf16[48,4096]{1,0:T(8,128)(2,1)S(1)} %fusion.4), channel_id=1, source_target_pairs={{2,0},{15,1},{4,2},{1,3},{6,4},{3,5},{8,6},{5,7},{10,8},{7,9},{12,... | collective-permute-start | bytes 1179656 | tf_op jit(solution)/shard_map/ppermute | solution.py:127
  128.2 5.8 %collective-permute-start.3 = (bf16[24,4096]{1,0:T(8,128)(2,1)S(1)}, bf16[24,4096]{1,0:T(8,128)(2,1)S(1)}, u32[]{:S(2)}, u32[]{:S(2)}) collective-permute-start(bf16[24,4096]{1,0:T(8,128)(2,1)S(1)} %slice.117), channel_id=1, source_target_pairs={{0,16},{16,0},{1,17},{17,1},{2,18},{18,2},{3,19},{19,3},{4,20},{20... | collective-permute-start | bytes 589832 | tf_op jit(solution)/shard_map/ppermute | solution.py:118
  133.4 1.5 %collective-permute-start.29 = (bf16[24,4096]{1,0:T(8,128)(2,1)S(1)}, bf16[24,4096]{1,0:T(8,128)(2,1)S(1)}, u32[]{:S(2)}, u32[]{:S(2)}) collective-permute-start(bf16[24,4096]{1,0:T(8,128)(2,1)S(1)} %slice.80), channel_id=1, source_target_pairs={{0,1},{1,0},{2,3},{3,2},{4,5},{5,4},{6,7},{7,6},{8,9},{9,8},{10,11... | collective-permute-start | bytes 589832 | tf_op jit(solution)/shard_map/ppermute | solution.py:128
  (7 other events, 58.8 us)
where the time goes:
time: 152 us; the launch traced here: 150 us
  waiting for transfers between devices  73.3 us (48%)
  starting transfers between devices  30.2 us (20%)
  Pallas kernels  19.4 us (13%)
  blocking collectives  14.2 us (9%)
  local copies, waits for them, and re-layouts  10.3 us (7%)
    ppermute x5, waiting for transfers between devices, gathered_sums(): own = jnp.concatenate([piece, lax.ppermute(piece, 'xl', SWAP)])  27 us
    ppermute x5, waiting for transfers between devices, gathered_sums(): crossed = lax.ppermute(half(total[count:]), 'xl', SWAP)  19.4 us
    ppermute x4, waiting for transfers between devices, gathered_sums(): block = lax.ppermute(block, RING, outward)  17 us
    pallas_call x5, Pallas kernels, project(): pl.pallas_call(expert_kernel, out_shape=(jax.ShapeDtypeStruct((count, fea...  15.2 us
    all_to_all x1, blocking collectives, local(): lax.all_to_all(results.reshape(groups, capacity, features), EXPERT, split...  14.2 us
    unnamed x22, local copies, waits for them, and re-layouts  8.48 us
    all_to_all x1, starting transfers between devices, local(): lax.all_to_all(outgoing.reshape(groups, capacity, features), EXPERT, spli...  7.38 us
    ppermute x3, starting transfers between devices, gathered_sums(): came = wide(lax.ppermute(half(running), RING, inward))  5.47 us
  transfers between devices with their start and end apart: 31, of which 16 were waited for; matrix products, arithmetic and copies ran while one was open for 1% of the time, Pallas kernels for 13%

commit v1 on v0

--- a/solution.py
+++ b/solution.py
@@ -103,15 +103,16 @@
     reach = length // 2
     pieces = [arrived]
     block = jnp.concatenate([arrived, lax.ppermute(arrived, "c", SWAP)])
-    for step in range(1, reach + 1):
-        if step == reach:
-            block = block[:size]
+    for _ in range(1, reach):
         block = lax.ppermute(block, RING, outward)
         pieces.append(block)
+    opposite = [(z, (z + reach) % length) for z in range(length)]
+    pieces.append(lax.ppermute(arrived, "z", opposite))
     sums = []
     for piece in pieces:
         count = piece.shape[0]
-        own = jnp.concatenate([piece, lax.ppermute(piece, "xl", SWAP)])
+        side = lax.ppermute(piece, "xl", SWAP)
+        own = jnp.concatenate([piece, side])
         other = lax.ppermute(own, "c", SWAP)
         keep, give = project(own, other, gate, up, down)
         total = keep + wide(lax.ppermute(give, "c", SWAP))

time: 152 us -> 150 us (0.987)
  waiting for transfers between devices: 73.3 us -> 57.9 us
  starting transfers between devices: 30.2 us -> 39 us
  local copies, waits for them, and re-layouts: 10.3 us -> 14.4 us
    ppermute x4 -> x3, waiting for transfers between devices: 17 us -> 8.24 us  [gathered_sums(): block = lax.ppermute(block, RING, outward)]
    ppermute x5 -> x6, starting transfers between devices: 3.65 us -> 10.6 us  [the longest x1 7.28 us: gathered_sums(): pieces.append(lax.ppermute(arrived, 'z', opposite))]
    unnamed x22, local copies, waits for them, and re-layouts: 8.48 us -> 12.5 us
    ppermute x5 -> x6, waiting for transfers between devices: 27 us -> 23.2 us  [the longest x5 23.2 us: gathered_sums(): side = lax.ppermute(piece, 'xl', SWAP)]
    ppermute x3, waiting for transfers between devices: 2.9 us -> 0.53 us  [gathered_sums(): came = wide(lax.ppermute(half(running), RING, inward))]
    ppermute x5, starting transfers between devices: 4.74 us -> 6.87 us  [gathered_sums(): crossed = lax.ppermute(half(total[count:]), 'xl', SWAP)]
    ppermute x5, starting transfers between devices: 2.41 us -> 0.81 us  [gathered_sums(): other = lax.ppermute(own, 'c', SWAP)]
where the time goes in v1:
time: 150 us; the launch traced here: 149 us
  waiting for transfers between devices  57.9 us (39%)
  starting transfers between devices  39 us (26%)
  Pallas kernels  19.5 us (13%)
  blocking collectives  14.9 us (10%)
  local copies, waits for them, and re-layouts  14.4 us (10%)
  other arithmetic  1.51 us (1%)
    ppermute x5, waiting for transfers between devices, gathered_sums(): side = lax.ppermute(piece, 'xl', SWAP)  23.2 us
    ppermute x5, waiting for transfers between devices, gathered_sums(): crossed = lax.ppermute(half(total[count:]), 'xl', SWAP)  19.4 us
    pallas_call x5, Pallas kernels, project(): pl.pallas_call(expert_kernel, out_shape=(jax.ShapeDtypeStruct((count, fea...  15.2 us
    all_to_all x1, blocking collectives, local(): lax.all_to_all(results.reshape(groups, capacity, features), EXPERT, split...  14.9 us
    unnamed x22, local copies, waits for them, and re-layouts  12.5 us
    ppermute x3, waiting for transfers between devices, gathered_sums(): block = lax.ppermute(block, RING, outward)  8.24 us
    all_to_all x1, starting transfers between devices, local(): lax.all_to_all(outgoing.reshape(groups, capacity, features), EXPERT, spli...  7.38 us
    ppermute x1, starting transfers between devices, gathered_sums(): pieces.append(lax.ppermute(arrived, 'z', opposite))  7.28 us
  transfers between devices with their start and end apart: 31, of which 16 were waited for; matrix products, arithmetic and copies ran while one was open for 1% of the time, Pallas kernels for 13%

profile of v1, /device:TPU:8, one launch (start us, length us, event | category | flops | bytes accessed | tf_op | source)
XLA Modules:
  0.0 148.6 jit_solution(12489192115944335069)
XLA Ops:
  2.5 7.4 %all-to-all-start = ((bf16[8,3,4096]{2,1,0:T(4,128)(2,1)}), bf16[8,3,4096]{2,1,0:T(4,128)(2,1)S(1)}, u32[]{:S(2)}, u32[]{:S(2)}) async-start(bf16[8,3,4096]{2,1,0:T(4,128)(2,1)} %reshape.54), calls=%async_computation | async-start | bytes 524288 | tf_op jit(solution)/shard_map/all_to_all | solution.py:154
  9.9 4.3 %load.1 = (bf16[448,4096]{1,0:T(8,128)(2,1)S(1)}, bf16[448,4096]{1,0:T(8,128)(2,1)S(1)}, bf16[448,4096]{1,0:T(8,128)(2,1)S(1)}) custom-call(bf16[448,4096]{1,0:T(8,128)(2,1)} %bitcast.13, bf16[448,4096]{1,0:T(8,128)(2,1)} %bitcast.14, bf16[448,4096]{1,0:T(8,128)(2,1)} %bitcast.15), custom_call_target="tpu_custom_call" | custom-call | tf_op jit(solution)/shard_map/load/pallas_call | solution.py:36
  14.2 1.8 %copy-done.1 = bf16[448,4096]{1,0:T(8,128)(2,1)} copy-done((bf16[448,4096]{1,0:T(8,128)(2,1)}, bf16[448,4096]{1,0:T(8,128)(2,1)S(1)}, u32[]{:S(2)}) %copy-start.1) | copy-done | bytes 3670040
  16.0 1.8 %copy-done.3 = bf16[448,4096]{1,0:T(8,128)(2,1)} copy-done((bf16[448,4096]{1,0:T(8,128)(2,1)}, bf16[448,4096]{1,0:T(8,128)(2,1)S(1)}, u32[]{:S(2)}) %copy-start.3) | copy-done | bytes 3670040
  17.8 1.9 %copy-done.5 = bf16[448,4096]{1,0:T(8,128)(2,1)} copy-done((bf16[448,4096]{1,0:T(8,128)(2,1)}, bf16[448,4096]{1,0:T(8,128)(2,1)S(1)}, u32[]{:S(2)}) %copy-start.5) | copy-done | bytes 3670040
  19.9 7.3 %collective-permute-start.20 = (bf16[24,4096]{1,0:T(8,128)(2,1)S(1)}, bf16[24,4096]{1,0:T(8,128)(2,1)S(1)}, u32[]{:S(2)}, u32[]{:S(2)}) collective-permute-start(bf16[24,4096]{1,0:T(8,128)(2,1)S(1)} %reshape.55), channel_id=1, source_target_pairs={{0,8},{2,10},{4,12},{6,14},{8,0},{10,2},{12,4},{14,6},{1,9},{3,11}... | collective-permute-start | bytes 589832 | tf_op jit(solution)/shard_map/ppermute | solution.py:110
  29.7 4.9 %collective-permute-done = bf16[24,4096]{1,0:T(8,128)(2,1)S(1)} collective-permute-done((bf16[24,4096]{1,0:T(8,128)(2,1)S(1)}, bf16[24,4096]{1,0:T(8,128)(2,1)S(1)}, u32[]{:S(2)}, u32[]{:S(2)}) %collective-permute-start) | collective-permute-done | bytes 196640 | tf_op jit(solution)/shard_map/ppermute | solution.py:114
  35.4 6.6 %collective-permute-done.21 = bf16[24,4096]{1,0:T(8,128)(2,1)S(1)} collective-permute-done((bf16[24,4096]{1,0:T(8,128)(2,1)S(1)}, bf16[24,4096]{1,0:T(8,128)(2,1)S(1)}, u32[]{:S(2)}, u32[]{:S(2)}) %collective-permute-start.21) | collective-permute-done | bytes 196640 | tf_op jit(solution)/shard_map/ppermute | solution.py:114
  42.1 1.9 %collective-permute-start.10 = (bf16[48,4096]{1,0:T(8,128)(2,1)S(1)}, bf16[48,4096]{1,0:T(8,128)(2,1)S(1)}, u32[]{:S(2)}, u32[]{:S(2)}) collective-permute-start(bf16[48,4096]{1,0:T(8,128)(2,1)S(1)} %collective-permute-done.5), channel_id=1, source_target_pairs={{0,2},{1,15},{2,4},{3,1},{4,6},{5,3},{6,8},{7,5},{8,10},{9,7},{10,... | collective-permute-start | bytes 1179656 | tf_op jit(solution)/shard_map/ppermute | solution.py:107
  44.7 2.0 %copy-done.2 = bf16[448,4096]{1,0:T(8,128)(2,1)S(1)} copy-done((bf16[448,4096]{1,0:T(8,128)(2,1)S(1)}, bf16[448,4096]{1,0:T(8,128)(2,1)}, u32[]{:S(2)}) %copy-start.2) | copy-done | bytes 3670040
  46.7 2.0 %copy-done.4 = bf16[448,4096]{1,0:T(8,128)(2,1)S(1)} copy-done((bf16[448,4096]{1,0:T(8,128)(2,1)S(1)}, bf16[448,4096]{1,0:T(8,128)(2,1)}, u32[]{:S(2)}) %copy-start.4) | copy-done | bytes 3670040
  48.7 2.0 %copy-done.6 = bf16[448,4096]{1,0:T(8,128)(2,1)S(1)} copy-done((bf16[448,4096]{1,0:T(8,128)(2,1)S(1)}, bf16[448,4096]{1,0:T(8,128)(2,1)}, u32[]{:S(2)}) %copy-start.6) | copy-done | bytes 3670040
  50.8 2.9 %expert.9 = (f32[48,4096]{1,0:T(8,128)S(1)}, bf16[48,4096]{1,0:T(8,128)(2,1)S(1)}) custom-call(bf16[48,4096]{1,0:T(8,128)(2,1)S(1)} %constant_dynamic-update-slice_fusion.8.own_ref, bf16[48,4096]{1,0:T(8,128)(2,1)S(1)} %collective-permute-done.22.other_ref, bf16[448,4096]{1,0:T(8,128)(2,1)S(1)} %copy-done.2, bf16[448,4096]{1,0:T(8,128)(2,1)S(1)} %copy-done.4, ...), custom_call_target="tpu_custom_call" | custom-call | flops 1056964608 | bytes 12976128 | tf_op jit(solution)/shard_map/expert/pallas_call | solution.py:72
  56.7 8.2 %collective-permute-done.15 = bf16[48,4096]{1,0:T(8,128)(2,1)S(1)} collective-permute-done((bf16[48,4096]{1,0:T(8,128)(2,1)S(1)}, bf16[48,4096]{1,0:T(8,128)(2,1)S(1)}, u32[]{:S(2)}, u32[]{:S(2)}) %collective-permute-start.15) | collective-permute-done | bytes 393248 | tf_op jit(solution)/shard_map/ppermute | solution.py:107
  65.6 10.8 %collective-permute-done.16 = bf16[48,4096]{1,0:T(8,128)(2,1)S(1)} collective-permute-done((bf16[48,4096]{1,0:T(8,128)(2,1)S(1)}, bf16[48,4096]{1,0:T(8,128)(2,1)S(1)}, u32[]{:S(2)}, u32[]{:S(2)}) %collective-permute-start.16) | collective-permute-done | bytes 393248 | tf_op jit(solution)/shard_map/ppermute | solution.py:114
  78.8 3.1 %expert.8 = (f32[96,4096]{1,0:T(8,128)S(1)}, bf16[96,4096]{1,0:T(8,128)(2,1)S(1)}) custom-call(bf16[96,4096]{1,0:T(8,128)(2,1)S(1)} %constant_dynamic-update-slice_fusion.6.own_ref, bf16[96,4096]{1,0:T(8,128)(2,1)S(1)} %collective-permute-done.17.other_ref, bf16[448,4096]{1,0:T(8,128)(2,1)S(1)} %copy-done.2, bf16[448,4096]{1,0:T(8,128)(2,1)S(1)} %copy-done.4, ...), custom_call_target="tpu_custom_call" | custom-call | flops 2113929216 | bytes 14942208 | tf_op jit(solution)/shard_map/expert/pallas_call | solution.py:72
  82.2 2.1 %collective-permute-done.24 = bf16[24,4096]{1,0:T(8,128)(2,1)S(1)} collective-permute-done((bf16[24,4096]{1,0:T(8,128)(2,1)S(1)}, bf16[24,4096]{1,0:T(8,128)(2,1)S(1)}, u32[]{:S(2)}, u32[]{:S(2)}) %collective-permute-start.24) | collective-permute-done | bytes 196640 | tf_op jit(solution)/shard_map/ppermute | solution.py:119
  84.3 2.6 %collective-permute-start.25 = (bf16[24,4096]{1,0:T(8,128)(2,1)S(1)}, bf16[24,4096]{1,0:T(8,128)(2,1)S(1)}, u32[]{:S(2)}, u32[]{:S(2)}) collective-permute-start(bf16[24,4096]{1,0:T(8,128)(2,1)S(1)} %fusion.5), channel_id=1, source_target_pairs={{2,0},{15,1},{4,2},{1,3},{6,4},{3,5},{8,6},{5,7},{10,8},{7,9},{12,... | collective-permute-start | bytes 589832 | tf_op jit(solution)/shard_map/ppermute | solution.py:123
  86.9 3.1 %expert.6 = (f32[96,4096]{1,0:T(8,128)S(1)}, bf16[96,4096]{1,0:T(8,128)(2,1)S(1)}) custom-call(bf16[96,4096]{1,0:T(8,128)(2,1)S(1)} %constant_dynamic-update-slice_fusion.2.own_ref, bf16[96,4096]{1,0:T(8,128)(2,1)S(1)} %collective-permute-done.7.other_ref, bf16[448,4096]{1,0:T(8,128)(2,1)S(1)} %copy-done.2, bf16[448,4096]{1,0:T(8,128)(2,1)S(1)} %copy-done.4, ...), custom_call_target="tpu_custom_call" | custom-call | flops 2113929216 | bytes 14942208 | tf_op jit(solution)/shard_map/expert/pallas_call | solution.py:72
  90.2 3.1 %expert.7 = (f32[96,4096]{1,0:T(8,128)S(1)}, bf16[96,4096]{1,0:T(8,128)(2,1)S(1)}) custom-call(bf16[96,4096]{1,0:T(8,128)(2,1)S(1)} %constant_dynamic-update-slice_fusion.4.own_ref, bf16[96,4096]{1,0:T(8,128)(2,1)S(1)} %collective-permute-done.12.other_ref, bf16[448,4096]{1,0:T(8,128)(2,1)S(1)} %copy-done.2, bf16[448,4096]{1,0:T(8,128)(2,1)S(1)} %copy-done.4, ...), custom_call_target="tpu_custom_call" | custom-call | flops 2113929216 | bytes 14942208 | tf_op jit(solution)/shard_map/expert/pallas_call | solution.py:72
  94.0 1.1 collective-permute-start.19
  96.0 1.1 collective-permute-start.14
  97.1 9.0 %collective-permute-done.19 = bf16[48,4096]{1,0:T(8,128)(2,1)S(1)} collective-permute-done((bf16[48,4096]{1,0:T(8,128)(2,1)S(1)}, bf16[48,4096]{1,0:T(8,128)(2,1)S(1)}, u32[]{:S(2)}, u32[]{:S(2)}) %collective-permute-start.19) | collective-permute-done | bytes 393248 | tf_op jit(solution)/shard_map/ppermute | solution.py:119
  107.4 1.8 %collective-permute-start.9 = (bf16[48,4096]{1,0:T(8,128)(2,1)S(1)}, bf16[48,4096]{1,0:T(8,128)(2,1)S(1)}, u32[]{:S(2)}, u32[]{:S(2)}) collective-permute-start(bf16[48,4096]{1,0:T(8,128)(2,1)S(1)} %slice.109), channel_id=1, source_target_pairs={{0,16},{16,0},{1,17},{17,1},{2,18},{18,2},{3,19},{19,3},{4,20},{20... | collective-permute-start | bytes 1179656 | tf_op jit(solution)/shard_map/ppermute | solution.py:119
  109.3 5.3 %collective-permute-done.14 = bf16[48,4096]{1,0:T(8,128)(2,1)S(1)} collective-permute-done((bf16[48,4096]{1,0:T(8,128)(2,1)S(1)}, bf16[48,4096]{1,0:T(8,128)(2,1)S(1)}, u32[]{:S(2)}, u32[]{:S(2)}) %collective-permute-start.14) | collective-permute-done | bytes 393248 | tf_op jit(solution)/shard_map/ppermute | solution.py:119
  114.7 1.7 %collective-permute-start.27 = (bf16[48,4096]{1,0:T(8,128)(2,1)S(1)}, bf16[48,4096]{1,0:T(8,128)(2,1)S(1)}, u32[]{:S(2)}, u32[]{:S(2)}) collective-permute-start(bf16[48,4096]{1,0:T(8,128)(2,1)S(1)} %fusion.2), channel_id=1, source_target_pairs={{2,0},{15,1},{4,2},{1,3},{6,4},{3,5},{8,6},{5,7},{10,8},{7,9},{12,... | collective-permute-start | bytes 1179656 | tf_op jit(solution)/shard_map/ppermute | solution.py:123
  116.5 2.9 %expert.5 = (f32[48,4096]{1,0:T(8,128)S(1)}, bf16[48,4096]{1,0:T(8,128)(2,1)S(1)}) custom-call(bf16[48,4096]{1,0:T(8,128)(2,1)S(1)} %constant_dynamic-update-slice_fusion.own_ref, bf16[48,4096]{1,0:T(8,128)(2,1)S(1)} %collective-permute-done.1.other_ref, bf16[448,4096]{1,0:T(8,128)(2,1)S(1)} %copy-done.2, bf16[448,4096]{1,0:T(8,128)(2,1)S(1)} %copy-done.4, ...), custom_call_target="tpu_custom_call" | custom-call | flops 1056964608 | bytes 12976128 | tf_op jit(solution)/shard_map/expert/pallas_call | solution.py:72
  119.5 2.5 %collective-permute-done.9 = bf16[48,4096]{1,0:T(8,128)(2,1)S(1)} collective-permute-done((bf16[48,4096]{1,0:T(8,128)(2,1)S(1)}, bf16[48,4096]{1,0:T(8,128)(2,1)S(1)}, u32[]{:S(2)}, u32[]{:S(2)}) %collective-permute-start.9) | collective-permute-done | bytes 393248 | tf_op jit(solution)/shard_map/ppermute | solution.py:119
  122.7 3.0 %collective-permute-start.28 = (bf16[48,4096]{1,0:T(8,128)(2,1)S(1)}, bf16[48,4096]{1,0:T(8,128)(2,1)S(1)}, u32[]{:S(2)}, u32[]{:S(2)}) collective-permute-start(bf16[48,4096]{1,0:T(8,128)(2,1)S(1)} %fusion.4), channel_id=1, source_target_pairs={{2,0},{15,1},{4,2},{1,3},{6,4},{3,5},{8,6},{5,7},{10,8},{7,9},{12,... | collective-permute-start | bytes 1179656 | tf_op jit(solution)/shard_map/ppermute | solution.py:128
  125.8 1.8 %collective-permute-start.3 = (bf16[24,4096]{1,0:T(8,128)(2,1)S(1)}, bf16[24,4096]{1,0:T(8,128)(2,1)S(1)}, u32[]{:S(2)}, u32[]{:S(2)}) collective-permute-start(bf16[24,4096]{1,0:T(8,128)(2,1)S(1)} %slice.112), channel_id=1, source_target_pairs={{0,16},{16,0},{1,17},{17,1},{2,18},{18,2},{3,19},{19,3},{4,20},{20... | collective-permute-start | bytes 589832 | tf_op jit(solution)/shard_map/ppermute | solution.py:119
  127.6 3.3 %collective-permute-done.28 = bf16[48,4096]{1,0:T(8,128)(2,1)S(1)} collective-permute-done((bf16[48,4096]{1,0:T(8,128)(2,1)S(1)}, bf16[48,4096]{1,0:T(8,128)(2,1)S(1)}, u32[]{:S(2)}, u32[]{:S(2)}) %collective-permute-start.28) | collective-permute-done | bytes 393248 | tf_op jit(solution)/shard_map/ppermute | solution.py:128
  132.7 14.9 %all_to_all.10 = bf16[8,3,4096]{2,1,0:T(4,128)(2,1)S(1)} all-to-all(bf16[8,3,4096]{2,1,0:T(4,128)(2,1)S(1)} %reshape.56), channel_id=1, replica_groups=mesh['xh'=2,'y'=4,'xl'=2,'z'=8,'c'=2] {'xh','y'}, dimensions={0} | all-to-all | bytes 393216 | tf_op jit(solution)/shard_map/all_to_all | solution.py:158
  (98 shorter events, 19.7 us)
Async XLA Ops:
  2.5 17.2 %all-to-all-start = ((bf16[8,3,4096]{2,1,0:T(4,128)(2,1)}), bf16[8,3,4096]{2,1,0:T(4,128)(2,1)S(1)}, u32[]{:S(2)}, u32[]{:S(2)}) async-start(bf16[8,3,4096]{2,1,0:T(4,128)(2,1)} %reshape.54), calls=%async_computation | async-start | bytes 524288 | tf_op jit(solution)/shard_map/all_to_all | solution.py:154
  19.9 14.8 %collective-permute-start.20 = (bf16[24,4096]{1,0:T(8,128)(2,1)S(1)}, bf16[24,4096]{1,0:T(8,128)(2,1)S(1)}, u32[]{:S(2)}, u32[]{:S(2)}) collective-permute-start(bf16[24,4096]{1,0:T(8,128)(2,1)S(1)} %reshape.55), channel_id=1, source_target_pairs={{0,8},{2,10},{4,12},{6,14},{8,0},{10,2},{12,4},{14,6},{1,9},{3,11}... | collective-permute-start | bytes 589832 | tf_op jit(solution)/shard_map/ppermute | solution.py:110
  27.2 1.4 collective-permute-start.4
  27.2 7.4 %collective-permute-start = (bf16[24,4096]{1,0:T(8,128)(2,1)S(1)}, bf16[24,4096]{1,0:T(8,128)(2,1)S(1)}, u32[]{:S(2)}, u32[]{:S(2)}) collective-permute-start(bf16[24,4096]{1,0:T(8,128)(2,1)S(1)} %reshape.55), channel_id=1, source_target_pairs={{0,16},{16,0},{1,17},{17,1},{2,18},{18,2},{3,19},{19,3},{4,20},{20... | collective-permute-start | bytes 589832 | tf_op jit(solution)/shard_map/ppermute | solution.py:114
  28.6 13.5 %collective-permute-start.5 = (bf16[48,4096]{1,0:T(8,128)(2,1)S(1)}, bf16[48,4096]{1,0:T(8,128)(2,1)S(1)}, u32[]{:S(2)}, u32[]{:S(2)}) collective-permute-start(bf16[48,4096]{1,0:T(8,128)(2,1)S(1)} %pad_maximum_fusion), channel_id=1, source_target_pairs={{0,2},{1,15},{2,4},{3,1},{4,6},{5,3},{6,8},{7,5},{8,10},{9,7},{10,... | collective-permute-start | bytes 1179656 | tf_op jit(solution)/shard_map/ppermute | solution.py:107
  34.6 81.8 %collective-permute-start.1 = (bf16[48,4096]{1,0:T(8,128)(2,1)S(1)}, bf16[48,4096]{1,0:T(8,128)(2,1)S(1)}, u32[]{:S(2)}, u32[]{:S(2)}) collective-permute-start(bf16[48,4096]{1,0:T(8,128)(2,1)S(1)} %constant_dynamic-update-slice_fusion.own_ref), channel_id=1, source_target_pairs={{0,1},{1,0},{2,3},{3,2},{4,5},{5,4},{6,7},{7,6},{8,9},{9,8},{10,11... | collective-permute-start | bytes 1179656 | tf_op jit(solution)/shard_map/ppermute | solution.py:116
  34.7 7.3 %collective-permute-start.21 = (bf16[24,4096]{1,0:T(8,128)(2,1)S(1)}, bf16[24,4096]{1,0:T(8,128)(2,1)S(1)}, u32[]{:S(2)}, u32[]{:S(2)}) collective-permute-start(bf16[24,4096]{1,0:T(8,128)(2,1)S(1)} %collective-permute-done.20), channel_id=1, source_target_pairs={{0,16},{16,0},{1,17},{17,1},{2,18},{18,2},{3,19},{19,3},{4,20},{20... | collective-permute-start | bytes 589832 | tf_op jit(solution)/shard_map/ppermute | solution.py:114
  42.0 2.6 %collective-permute-start.22 = (bf16[48,4096]{1,0:T(8,128)(2,1)S(1)}, bf16[48,4096]{1,0:T(8,128)(2,1)S(1)}, u32[]{:S(2)}, u32[]{:S(2)}) collective-permute-start(bf16[48,4096]{1,0:T(8,128)(2,1)S(1)} %constant_dynamic-update-slice_fusion.8.own_ref), channel_id=1, source_target_pairs={{0,1},{1,0},{2,3},{3,2},{4,5},{5,4},{6,7},{7,6},{8,9},{9,8},{10,11... | collective-permute-start | bytes 1179656 | tf_op jit(solution)/shard_map/ppermute | solution.py:116
  42.1 13.8 %collective-permute-start.10 = (bf16[48,4096]{1,0:T(8,128)(2,1)S(1)}, bf16[48,4096]{1,0:T(8,128)(2,1)S(1)}, u32[]{:S(2)}, u32[]{:S(2)}) collective-permute-start(bf16[48,4096]{1,0:T(8,128)(2,1)S(1)} %collective-permute-done.5), channel_id=1, source_target_pairs={{0,2},{1,15},{2,4},{3,1},{4,6},{5,3},{6,8},{7,5},{8,10},{9,7},{10,... | collective-permute-start | bytes 1179656 | tf_op jit(solution)/shard_map/ppermute | solution.py:107
  44.0 11.7 %collective-permute-start.6 = (bf16[48,4096]{1,0:T(8,128)(2,1)S(1)}, bf16[48,4096]{1,0:T(8,128)(2,1)S(1)}, u32[]{:S(2)}, u32[]{:S(2)}) collective-permute-start(bf16[48,4096]{1,0:T(8,128)(2,1)S(1)} %collective-permute-done.5), channel_id=1, source_target_pairs={{0,16},{16,0},{1,17},{17,1},{2,18},{18,2},{3,19},{19,3},{4,20},{20... | collective-permute-start | bytes 1179656 | tf_op jit(solution)/shard_map/ppermute | solution.py:114
  53.7 22.9 %collective-permute-start.23 = (bf16[48,4096]{1,0:T(8,128)(2,1)S(1)}, bf16[48,4096]{1,0:T(8,128)(2,1)S(1)}, u32[]{:S(2)}, u32[]{:S(2)}) collective-permute-start(bf16[48,4096]{1,0:T(8,128)(2,1)S(1)} %get-tuple-element.30), channel_id=1, source_target_pairs={{0,1},{1,0},{2,3},{3,2},{4,5},{5,4},{6,7},{7,6},{8,9},{9,8},{10,11... | collective-permute-start | bytes 1179656 | tf_op jit(solution)/shard_map/ppermute | solution.py:118
  55.7 31.2 %collective-permute-start.7 = (bf16[96,4096]{1,0:T(8,128)(2,1)S(1)}, bf16[96,4096]{1,0:T(8,128)(2,1)S(1)}, u32[]{:S(2)}, u32[]{:S(2)}) collective-permute-start(bf16[96,4096]{1,0:T(8,128)(2,1)S(1)} %constant_dynamic-update-slice_fusion.2.own_ref), channel_id=1, source_target_pairs={{0,1},{1,0},{2,3},{3,2},{4,5},{5,4},{6,7},{7,6},{8,9},{9,8},{10,11... | collective-permute-start | bytes 2359304 | tf_op jit(solution)/shard_map/ppermute | solution.py:116
  56.0 9.0 %collective-permute-start.15 = (bf16[48,4096]{1,0:T(8,128)(2,1)S(1)}, bf16[48,4096]{1,0:T(8,128)(2,1)S(1)}, u32[]{:S(2)}, u32[]{:S(2)}) collective-permute-start(bf16[48,4096]{1,0:T(8,128)(2,1)S(1)} %collective-permute-done.10), channel_id=1, source_target_pairs={{0,2},{1,15},{2,4},{3,1},{4,6},{5,3},{6,8},{7,5},{8,10},{9,7},{10,... | collective-permute-start | bytes 1179656 | tf_op jit(solution)/shard_map/ppermute | solution.py:107
  56.0 21.7 %collective-permute-start.11 = (bf16[48,4096]{1,0:T(8,128)(2,1)S(1)}, bf16[48,4096]{1,0:T(8,128)(2,1)S(1)}, u32[]{:S(2)}, u32[]{:S(2)}) collective-permute-start(bf16[48,4096]{1,0:T(8,128)(2,1)S(1)} %collective-permute-done.10), channel_id=1, source_target_pairs={{0,16},{16,0},{1,17},{17,1},{2,18},{18,2},{3,19},{19,3},{4,20},{20... | collective-permute-start | bytes 1179656 | tf_op jit(solution)/shard_map/ppermute | solution.py:114
  64.9 11.5 %collective-permute-start.16 = (bf16[48,4096]{1,0:T(8,128)(2,1)S(1)}, bf16[48,4096]{1,0:T(8,128)(2,1)S(1)}, u32[]{:S(2)}, u32[]{:S(2)}) collective-permute-start(bf16[48,4096]{1,0:T(8,128)(2,1)S(1)} %collective-permute-done.15), channel_id=1, source_target_pairs={{0,16},{16,0},{1,17},{17,1},{2,18},{18,2},{3,19},{19,3},{4,20},{20... | collective-permute-start | bytes 1179656 | tf_op jit(solution)/shard_map/ppermute | solution.py:114
  76.5 2.4 %collective-permute-start.17 = (bf16[96,4096]{1,0:T(8,128)(2,1)S(1)}, bf16[96,4096]{1,0:T(8,128)(2,1)S(1)}, u32[]{:S(2)}, u32[]{:S(2)}) collective-permute-start(bf16[96,4096]{1,0:T(8,128)(2,1)S(1)} %constant_dynamic-update-slice_fusion.6.own_ref), channel_id=1, source_target_pairs={{0,1},{1,0},{2,3},{3,2},{4,5},{5,4},{6,7},{7,6},{8,9},{9,8},{10,11... | collective-permute-start | bytes 2359304 | tf_op jit(solution)/shard_map/ppermute | solution.py:116
  76.7 7.6 %collective-permute-start.24 = (bf16[24,4096]{1,0:T(8,128)(2,1)S(1)}, bf16[24,4096]{1,0:T(8,128)(2,1)S(1)}, u32[]{:S(2)}, u32[]{:S(2)}) collective-permute-start(bf16[24,4096]{1,0:T(8,128)(2,1)S(1)} %slice.111), channel_id=1, source_target_pairs={{0,16},{16,0},{1,17},{17,1},{2,18},{18,2},{3,19},{19,3},{4,20},{20... | collective-permute-start | bytes 589832 | tf_op jit(solution)/shard_map/ppermute | solution.py:119
  77.6 12.5 %collective-permute-start.12 = (bf16[96,4096]{1,0:T(8,128)(2,1)S(1)}, bf16[96,4096]{1,0:T(8,128)(2,1)S(1)}, u32[]{:S(2)}, u32[]{:S(2)}) collective-permute-start(bf16[96,4096]{1,0:T(8,128)(2,1)S(1)} %constant_dynamic-update-slice_fusion.4.own_ref), channel_id=1, source_target_pairs={{0,1},{1,0},{2,3},{3,2},{4,5},{5,4},{6,7},{7,6},{8,9},{9,8},{10,11... | collective-permute-start | bytes 2359304 | tf_op jit(solution)/shard_map/ppermute | solution.py:116
  82.0 11.9 %collective-permute-start.18 = (bf16[96,4096]{1,0:T(8,128)(2,1)S(1)}, bf16[96,4096]{1,0:T(8,128)(2,1)S(1)}, u32[]{:S(2)}, u32[]{:S(2)}) collective-permute-start(bf16[96,4096]{1,0:T(8,128)(2,1)S(1)} %get-tuple-element.28), channel_id=1, source_target_pairs={{0,1},{1,0},{2,3},{3,2},{4,5},{5,4},{6,7},{7,6},{8,9},{9,8},{10,11... | collective-permute-start | bytes 2359304 | tf_op jit(solution)/shard_map/ppermute | solution.py:118
  84.3 21.9 %collective-permute-start.25 = (bf16[24,4096]{1,0:T(8,128)(2,1)S(1)}, bf16[24,4096]{1,0:T(8,128)(2,1)S(1)}, u32[]{:S(2)}, u32[]{:S(2)}) collective-permute-start(bf16[24,4096]{1,0:T(8,128)(2,1)S(1)} %fusion.5), channel_id=1, source_target_pairs={{2,0},{15,1},{4,2},{1,3},{6,4},{3,5},{8,6},{5,7},{10,8},{7,9},{12,... | collective-permute-start | bytes 589832 | tf_op jit(solution)/shard_map/ppermute | solution.py:123
  90.0 17.2 %collective-permute-start.8 = (bf16[96,4096]{1,0:T(8,128)(2,1)S(1)}, bf16[96,4096]{1,0:T(8,128)(2,1)S(1)}, u32[]{:S(2)}, u32[]{:S(2)}) collective-permute-start(bf16[96,4096]{1,0:T(8,128)(2,1)S(1)} %get-tuple-element.24), channel_id=1, source_target_pairs={{0,1},{1,0},{2,3},{3,2},{4,5},{5,4},{6,7},{7,6},{8,9},{9,8},{10,11... | collective-permute-start | bytes 2359304 | tf_op jit(solution)/shard_map/ppermute | solution.py:118
  93.3 2.5 %collective-permute-start.13 = (bf16[96,4096]{1,0:T(8,128)(2,1)S(1)}, bf16[96,4096]{1,0:T(8,128)(2,1)S(1)}, u32[]{:S(2)}, u32[]{:S(2)}) collective-permute-start(bf16[96,4096]{1,0:T(8,128)(2,1)S(1)} %get-tuple-element.26), channel_id=1, source_target_pairs={{0,1},{1,0},{2,3},{3,2},{4,5},{5,4},{6,7},{7,6},{8,9},{9,8},{10,11... | collective-permute-start | bytes 2359304 | tf_op jit(solution)/shard_map/ppermute | solution.py:118
  94.0 12.1 %collective-permute-start.19 = (bf16[48,4096]{1,0:T(8,128)(2,1)S(1)}, bf16[48,4096]{1,0:T(8,128)(2,1)S(1)}, u32[]{:S(2)}, u32[]{:S(2)}) collective-permute-start(bf16[48,4096]{1,0:T(8,128)(2,1)S(1)} %slice.107), channel_id=1, source_target_pairs={{0,16},{16,0},{1,17},{17,1},{2,18},{18,2},{3,19},{19,3},{4,20},{20... | collective-permute-start | bytes 1179656 | tf_op jit(solution)/shard_map/ppermute | solution.py:119
  96.0 18.6 %collective-permute-start.14 = (bf16[48,4096]{1,0:T(8,128)(2,1)S(1)}, bf16[48,4096]{1,0:T(8,128)(2,1)S(1)}, u32[]{:S(2)}, u32[]{:S(2)}) collective-permute-start(bf16[48,4096]{1,0:T(8,128)(2,1)S(1)} %slice.108), channel_id=1, source_target_pairs={{0,16},{16,0},{1,17},{17,1},{2,18},{18,2},{3,19},{19,3},{4,20},{20... | collective-permute-start | bytes 1179656 | tf_op jit(solution)/shard_map/ppermute | solution.py:119
  106.3 8.2 %collective-permute-start.26 = (bf16[48,4096]{1,0:T(8,128)(2,1)S(1)}, bf16[48,4096]{1,0:T(8,128)(2,1)S(1)}, u32[]{:S(2)}, u32[]{:S(2)}) collective-permute-start(bf16[48,4096]{1,0:T(8,128)(2,1)S(1)} %pad_maximum_fusion.1), channel_id=1, source_target_pairs={{2,0},{15,1},{4,2},{1,3},{6,4},{3,5},{8,6},{5,7},{10,8},{7,9},{12,... | collective-permute-start | bytes 1179656 | tf_op jit(solution)/shard_map/ppermute | solution.py:123
  107.4 14.6 %collective-permute-start.9 = (bf16[48,4096]{1,0:T(8,128)(2,1)S(1)}, bf16[48,4096]{1,0:T(8,128)(2,1)S(1)}, u32[]{:S(2)}, u32[]{:S(2)}) collective-permute-start(bf16[48,4096]{1,0:T(8,128)(2,1)S(1)} %slice.109), channel_id=1, source_target_pairs={{0,16},{16,0},{1,17},{17,1},{2,18},{18,2},{3,19},{19,3},{4,20},{20... | collective-permute-start | bytes 1179656 | tf_op jit(solution)/shard_map/ppermute | solution.py:119
  114.7 7.9 %collective-permute-start.27 = (bf16[48,4096]{1,0:T(8,128)(2,1)S(1)}, bf16[48,4096]{1,0:T(8,128)(2,1)S(1)}, u32[]{:S(2)}, u32[]{:S(2)}) collective-permute-start(bf16[48,4096]{1,0:T(8,128)(2,1)S(1)} %fusion.2), channel_id=1, source_target_pairs={{2,0},{15,1},{4,2},{1,3},{6,4},{3,5},{8,6},{5,7},{10,8},{7,9},{12,... | collective-permute-start | bytes 1179656 | tf_op jit(solution)/shard_map/ppermute | solution.py:123
  119.4 6.3 %collective-permute-start.2 = (bf16[48,4096]{1,0:T(8,128)(2,1)S(1)}, bf16[48,4096]{1,0:T(8,128)(2,1)S(1)}, u32[]{:S(2)}, u32[]{:S(2)}) collective-permute-start(bf16[48,4096]{1,0:T(8,128)(2,1)S(1)} %get-tuple-element.22), channel_id=1, source_target_pairs={{0,1},{1,0},{2,3},{3,2},{4,5},{5,4},{6,7},{7,6},{8,9},{9,8},{10,11... | collective-permute-start | bytes 1179656 | tf_op jit(solution)/shard_map/ppermute | solution.py:118
  122.7 8.2 %collective-permute-start.28 = (bf16[48,4096]{1,0:T(8,128)(2,1)S(1)}, bf16[48,4096]{1,0:T(8,128)(2,1)S(1)}, u32[]{:S(2)}, u32[]{:S(2)}) collective-permute-start(bf16[48,4096]{1,0:T(8,128)(2,1)S(1)} %fusion.4), channel_id=1, source_target_pairs={{2,0},{15,1},{4,2},{1,3},{6,4},{3,5},{8,6},{5,7},{10,8},{7,9},{12,... | collective-permute-start | bytes 1179656 | tf_op jit(solution)/shard_map/ppermute | solution.py:128
  125.7 22.0 %copy-start.7 = (f32[8,2]{0,1:T(2,128)S(1)}, f32[8,2]{0,1:T(2,128)}, u32[]{:S(2)}) copy-start(f32[8,2]{0,1:T(2,128)} %param.8) | copy-start | bytes 196
  125.8 5.8 %collective-permute-start.3 = (bf16[24,4096]{1,0:T(8,128)(2,1)S(1)}, bf16[24,4096]{1,0:T(8,128)(2,1)S(1)}, u32[]{:S(2)}, u32[]{:S(2)}) collective-permute-start(bf16[24,4096]{1,0:T(8,128)(2,1)S(1)} %slice.112), channel_id=1, source_target_pairs={{0,16},{16,0},{1,17},{17,1},{2,18},{18,2},{3,19},{19,3},{4,20},{20... | collective-permute-start | bytes 589832 | tf_op jit(solution)/shard_map/ppermute | solution.py:119
  130.9 1.5 %collective-permute-start.29 = (bf16[24,4096]{1,0:T(8,128)(2,1)S(1)}, bf16[24,4096]{1,0:T(8,128)(2,1)S(1)}, u32[]{:S(2)}, u32[]{:S(2)}) collective-permute-start(bf16[24,4096]{1,0:T(8,128)(2,1)S(1)} %slice.75), channel_id=1, source_target_pairs={{0,1},{1,0},{2,3},{3,2},{4,5},{5,4},{6,7},{7,6},{8,9},{9,8},{10,11... | collective-permute-start | bytes 589832 | tf_op jit(solution)/shard_map/ppermute | solution.py:129
  (7 other events, 13.1 us)

commit v2 on v0

--- a/solution.py
+++ b/solution.py
@@ -114,9 +114,10 @@
         own = jnp.concatenate([piece, lax.ppermute(piece, "xl", SWAP)])
         other = lax.ppermute(own, "c", SWAP)
         keep, give = project(own, other, gate, up, down)
-        total = keep + wide(lax.ppermute(give, "c", SWAP))
-        crossed = lax.ppermute(half(total[count:]), "xl", SWAP)
-        sums.append(total[:count] + wide(crossed))
+        taken = lax.ppermute(give, "c", SWAP)
+        crossing = half(keep[count:] + wide(taken[count:]))
+        crossed = lax.ppermute(crossing, "xl", SWAP)
+        sums.append(keep[:count] + wide(taken[:count]) + wide(crossed))
     running = sums[reach]
     for step in range(reach - 1, 0, -1):
         came = wide(lax.ppermute(half(running), RING, inward))

time: 152 us -> 152 us (level)
  no operation moved by 1% of the time
where the time goes in v2:
time: 152 us; the launch traced here: 150 us
  waiting for transfers between devices  73.5 us (48%)
  starting transfers between devices  30.3 us (20%)
  Pallas kernels  19.4 us (13%)
  blocking collectives  14.2 us (9%)
  local copies, waits for them, and re-layouts  10.2 us (7%)
    ppermute x5, waiting for transfers between devices, gathered_sums(): own = jnp.concatenate([piece, lax.ppermute(piece, 'xl', SWAP)])  27 us
    ppermute x5, waiting for transfers between devices, gathered_sums(): crossed = lax.ppermute(crossing, 'xl', SWAP)  19.5 us
    ppermute x4, waiting for transfers between devices, gathered_sums(): block = lax.ppermute(block, RING, outward)  17 us
    pallas_call x5, Pallas kernels, project(): pl.pallas_call(expert_kernel, out_shape=(jax.ShapeDtypeStruct((count, fea...  15.2 us
    all_to_all x1, blocking collectives, local(): lax.all_to_all(results.reshape(groups, capacity, features), EXPERT, split...  14.2 us
    unnamed x22, local copies, waits for them, and re-layouts  8.48 us
    all_to_all x1, starting transfers between devices, local(): lax.all_to_all(outgoing.reshape(groups, capacity, features), EXPERT, spli...  7.38 us
    ppermute x3, starting transfers between devices, gathered_sums(): came = wide(lax.ppermute(half(running), RING, inward))  5.51 us
  transfers between devices with their start and end apart: 31, of which 16 were waited for; matrix products, arithmetic and copies ran while one was open for 1% of the time, Pallas kernels for 13%

profile of v2, /device:TPU:8, one launch (start us, length us, event | category | flops | bytes accessed | tf_op | source)
XLA Modules:
  0.0 150.5 jit_solution(7783201538324256515)
XLA Ops:
  2.5 7.4 %all-to-all-start = ((bf16[8,3,4096]{2,1,0:T(4,128)(2,1)}), bf16[8,3,4096]{2,1,0:T(4,128)(2,1)S(1)}, u32[]{:S(2)}, u32[]{:S(2)}) async-start(bf16[8,3,4096]{2,1,0:T(4,128)(2,1)} %reshape.54), calls=%async_computation | async-start | bytes 524288 | tf_op jit(solution)/shard_map/all_to_all | solution.py:154
  9.9 4.3 %load.1 = (bf16[448,4096]{1,0:T(8,128)(2,1)S(1)}, bf16[448,4096]{1,0:T(8,128)(2,1)S(1)}, bf16[448,4096]{1,0:T(8,128)(2,1)S(1)}) custom-call(bf16[448,4096]{1,0:T(8,128)(2,1)} %bitcast.13, bf16[448,4096]{1,0:T(8,128)(2,1)} %bitcast.14, bf16[448,4096]{1,0:T(8,128)(2,1)} %bitcast.15), custom_call_target="tpu_custom_call" | custom-call | tf_op jit(solution)/shard_map/load/pallas_call | solution.py:36
  14.2 1.8 %copy-done.1 = bf16[448,4096]{1,0:T(8,128)(2,1)} copy-done((bf16[448,4096]{1,0:T(8,128)(2,1)}, bf16[448,4096]{1,0:T(8,128)(2,1)S(1)}, u32[]{:S(2)}) %copy-start.1) | copy-done | bytes 3670040
  16.0 1.9 %copy-done.3 = bf16[448,4096]{1,0:T(8,128)(2,1)} copy-done((bf16[448,4096]{1,0:T(8,128)(2,1)}, bf16[448,4096]{1,0:T(8,128)(2,1)S(1)}, u32[]{:S(2)}) %copy-start.3) | copy-done | bytes 3670040
  17.9 1.8 %copy-done.5 = bf16[448,4096]{1,0:T(8,128)(2,1)} copy-done((bf16[448,4096]{1,0:T(8,128)(2,1)}, bf16[448,4096]{1,0:T(8,128)(2,1)S(1)}, u32[]{:S(2)}) %copy-start.5) | copy-done | bytes 3670040
  21.4 2.0 %collective-permute-start.5 = (bf16[48,4096]{1,0:T(8,128)(2,1)S(1)}, bf16[48,4096]{1,0:T(8,128)(2,1)S(1)}, u32[]{:S(2)}, u32[]{:S(2)}) collective-permute-start(bf16[48,4096]{1,0:T(8,128)(2,1)S(1)} %pad_maximum_fusion), channel_id=1, source_target_pairs={{0,2},{1,15},{2,4},{3,1},{4,6},{5,3},{6,8},{7,5},{8,10},{9,7},{10,... | collective-permute-start | bytes 1179656 | tf_op jit(solution)/shard_map/ppermute | solution.py:109
  23.4 4.0 %collective-permute-done = bf16[24,4096]{1,0:T(8,128)(2,1)S(1)} collective-permute-done((bf16[24,4096]{1,0:T(8,128)(2,1)S(1)}, bf16[24,4096]{1,0:T(8,128)(2,1)S(1)}, u32[]{:S(2)}, u32[]{:S(2)}) %collective-permute-start) | collective-permute-done | bytes 196640 | tf_op jit(solution)/shard_map/ppermute | solution.py:114
  27.5 5.6 %collective-permute-done.5 = bf16[48,4096]{1,0:T(8,128)(2,1)S(1)} collective-permute-done((bf16[48,4096]{1,0:T(8,128)(2,1)S(1)}, bf16[48,4096]{1,0:T(8,128)(2,1)S(1)}, u32[]{:S(2)}, u32[]{:S(2)}) %collective-permute-start.5) | collective-permute-done | bytes 393248 | tf_op jit(solution)/shard_map/ppermute | solution.py:109
  33.9 10.3 %collective-permute-done.6 = bf16[48,4096]{1,0:T(8,128)(2,1)S(1)} collective-permute-done((bf16[48,4096]{1,0:T(8,128)(2,1)S(1)}, bf16[48,4096]{1,0:T(8,128)(2,1)S(1)}, u32[]{:S(2)}, u32[]{:S(2)}) %collective-permute-start.6) | collective-permute-done | bytes 393248 | tf_op jit(solution)/shard_map/ppermute | solution.py:114
  45.8 8.2 %collective-permute-done.15 = bf16[48,4096]{1,0:T(8,128)(2,1)S(1)} collective-permute-done((bf16[48,4096]{1,0:T(8,128)(2,1)S(1)}, bf16[48,4096]{1,0:T(8,128)(2,1)S(1)}, u32[]{:S(2)}, u32[]{:S(2)}) %collective-permute-start.15) | collective-permute-done | bytes 393248 | tf_op jit(solution)/shard_map/ppermute | solution.py:109
  54.2 2.2 %collective-permute-done.11 = bf16[48,4096]{1,0:T(8,128)(2,1)S(1)} collective-permute-done((bf16[48,4096]{1,0:T(8,128)(2,1)S(1)}, bf16[48,4096]{1,0:T(8,128)(2,1)S(1)}, u32[]{:S(2)}, u32[]{:S(2)}) %collective-permute-start.11) | collective-permute-done | bytes 393248 | tf_op jit(solution)/shard_map/ppermute | solution.py:114
  57.8 3.2 %collective-permute-done.20 = bf16[24,4096]{1,0:T(8,128)(2,1)S(1)} collective-permute-done((bf16[24,4096]{1,0:T(8,128)(2,1)S(1)}, bf16[24,4096]{1,0:T(8,128)(2,1)S(1)}, u32[]{:S(2)}, u32[]{:S(2)}) %collective-permute-start.20) | collective-permute-done | bytes 196640 | tf_op jit(solution)/shard_map/ppermute | solution.py:109
  61.8 10.6 %collective-permute-done.21 = bf16[24,4096]{1,0:T(8,128)(2,1)S(1)} collective-permute-done((bf16[24,4096]{1,0:T(8,128)(2,1)S(1)}, bf16[24,4096]{1,0:T(8,128)(2,1)S(1)}, u32[]{:S(2)}, u32[]{:S(2)}) %collective-permute-start.21) | collective-permute-done | bytes 196640 | tf_op jit(solution)/shard_map/ppermute | solution.py:114
  73.3 0.9 collective-permute-done.22.other_ref
  74.2 2.0 %copy-done.6 = bf16[448,4096]{1,0:T(8,128)(2,1)S(1)} copy-done((bf16[448,4096]{1,0:T(8,128)(2,1)S(1)}, bf16[448,4096]{1,0:T(8,128)(2,1)}, u32[]{:S(2)}) %copy-start.6) | copy-done | bytes 3670040
  76.2 2.9 %expert.9 = (f32[48,4096]{1,0:T(8,128)S(1)}, bf16[48,4096]{1,0:T(8,128)(2,1)S(1)}) custom-call(bf16[48,4096]{1,0:T(8,128)(2,1)S(1)} %constant_dynamic-update-slice_fusion.8.own_ref, bf16[48,4096]{1,0:T(8,128)(2,1)S(1)} %collective-permute-done.22.other_ref, bf16[448,4096]{1,0:T(8,128)(2,1)S(1)} %copy-done.2, bf16[448,4096]{1,0:T(8,128)(2,1)S(1)} %copy-done.4, ...), custom_call_target="tpu_custom_call" | custom-call | flops 1056964608 | bytes 12976128 | tf_op jit(solution)/shard_map/expert/pallas_call | solution.py:72
  79.4 3.1 %expert.6 = (f32[96,4096]{1,0:T(8,128)S(1)}, bf16[96,4096]{1,0:T(8,128)(2,1)S(1)}) custom-call(bf16[96,4096]{1,0:T(8,128)(2,1)S(1)} %constant_dynamic-update-slice_fusion.2.own_ref, bf16[96,4096]{1,0:T(8,128)(2,1)S(1)} %collective-permute-done.7.other_ref, bf16[448,4096]{1,0:T(8,128)(2,1)S(1)} %copy-done.2, bf16[448,4096]{1,0:T(8,128)(2,1)S(1)} %copy-done.4, ...), custom_call_target="tpu_custom_call" | custom-call | flops 2113929216 | bytes 14942208 | tf_op jit(solution)/shard_map/expert/pallas_call | solution.py:72
  83.0 3.1 %expert.7 = (f32[96,4096]{1,0:T(8,128)S(1)}, bf16[96,4096]{1,0:T(8,128)(2,1)S(1)}) custom-call(bf16[96,4096]{1,0:T(8,128)(2,1)S(1)} %constant_dynamic-update-slice_fusion.4.own_ref, bf16[96,4096]{1,0:T(8,128)(2,1)S(1)} %collective-permute-done.12.other_ref, bf16[448,4096]{1,0:T(8,128)(2,1)S(1)} %copy-done.2, bf16[448,4096]{1,0:T(8,128)(2,1)S(1)} %copy-done.4, ...), custom_call_target="tpu_custom_call" | custom-call | flops 2113929216 | bytes 14942208 | tf_op jit(solution)/shard_map/expert/pallas_call | solution.py:72
  87.2 3.1 %expert.8 = (f32[96,4096]{1,0:T(8,128)S(1)}, bf16[96,4096]{1,0:T(8,128)(2,1)S(1)}) custom-call(bf16[96,4096]{1,0:T(8,128)(2,1)S(1)} %constant_dynamic-update-slice_fusion.6.own_ref, bf16[96,4096]{1,0:T(8,128)(2,1)S(1)} %collective-permute-done.17.other_ref, bf16[448,4096]{1,0:T(8,128)(2,1)S(1)} %copy-done.2, bf16[448,4096]{1,0:T(8,128)(2,1)S(1)} %copy-done.4, ...), custom_call_target="tpu_custom_call" | custom-call | flops 2113929216 | bytes 14942208 | tf_op jit(solution)/shard_map/expert/pallas_call | solution.py:72
  90.5 3.2 %collective-permute-done.24 = bf16[24,4096]{1,0:T(8,128)(2,1)S(1)} collective-permute-done((bf16[24,4096]{1,0:T(8,128)(2,1)S(1)}, bf16[24,4096]{1,0:T(8,128)(2,1)S(1)}, u32[]{:S(2)}, u32[]{:S(2)}) %collective-permute-start.24) | collective-permute-done | bytes 196640 | tf_op jit(solution)/shard_map/ppermute | solution.py:119
  93.7 2.5 %collective-permute-start.25 = (bf16[24,4096]{1,0:T(8,128)(2,1)S(1)}, bf16[24,4096]{1,0:T(8,128)(2,1)S(1)}, u32[]{:S(2)}, u32[]{:S(2)}) collective-permute-start(bf16[24,4096]{1,0:T(8,128)(2,1)S(1)} %add_convert_fusion.6), channel_id=1, source_target_pairs={{2,0},{15,1},{4,2},{1,3},{6,4},{3,5},{8,6},{5,7},{10,8},{7,9},{12,... | collective-permute-start | bytes 589832 | tf_op jit(solution)/shard_map/ppermute | solution.py:123
  97.2 1.3 collective-permute-start.14
  98.5 9.8 %collective-permute-done.19 = bf16[48,4096]{1,0:T(8,128)(2,1)S(1)} collective-permute-done((bf16[48,4096]{1,0:T(8,128)(2,1)S(1)}, bf16[48,4096]{1,0:T(8,128)(2,1)S(1)}, u32[]{:S(2)}, u32[]{:S(2)}) %collective-permute-start.19) | collective-permute-done | bytes 393248 | tf_op jit(solution)/shard_map/ppermute | solution.py:119
  108.5 1.1 collective-permute-start.26
  110.6 6.2 %collective-permute-done.14 = bf16[48,4096]{1,0:T(8,128)(2,1)S(1)} collective-permute-done((bf16[48,4096]{1,0:T(8,128)(2,1)S(1)}, bf16[48,4096]{1,0:T(8,128)(2,1)S(1)}, u32[]{:S(2)}, u32[]{:S(2)}) %collective-permute-start.14) | collective-permute-done | bytes 393248 | tf_op jit(solution)/shard_map/ppermute | solution.py:119
  116.9 2.0 %collective-permute-start.27 = (bf16[48,4096]{1,0:T(8,128)(2,1)S(1)}, bf16[48,4096]{1,0:T(8,128)(2,1)S(1)}, u32[]{:S(2)}, u32[]{:S(2)}) collective-permute-start(bf16[48,4096]{1,0:T(8,128)(2,1)S(1)} %add_convert_fusion.1), channel_id=1, source_target_pairs={{2,0},{15,1},{4,2},{1,3},{6,4},{3,5},{8,6},{5,7},{10,8},{7,9},{12,... | collective-permute-start | bytes 1179656 | tf_op jit(solution)/shard_map/ppermute | solution.py:123
  118.9 2.9 %expert.5 = (f32[48,4096]{1,0:T(8,128)S(1)}, bf16[48,4096]{1,0:T(8,128)(2,1)S(1)}) custom-call(bf16[48,4096]{1,0:T(8,128)(2,1)S(1)} %constant_dynamic-update-slice_fusion.own_ref, bf16[48,4096]{1,0:T(8,128)(2,1)S(1)} %collective-permute-done.1.other_ref, bf16[448,4096]{1,0:T(8,128)(2,1)S(1)} %copy-done.2, bf16[448,4096]{1,0:T(8,128)(2,1)S(1)} %copy-done.4, ...), custom_call_target="tpu_custom_call" | custom-call | flops 1056964608 | bytes 12976128 | tf_op jit(solution)/shard_map/expert/pallas_call | solution.py:72
  121.9 2.9 %collective-permute-done.27 = bf16[48,4096]{1,0:T(8,128)(2,1)S(1)} collective-permute-done((bf16[48,4096]{1,0:T(8,128)(2,1)S(1)}, bf16[48,4096]{1,0:T(8,128)(2,1)S(1)}, u32[]{:S(2)}, u32[]{:S(2)}) %collective-permute-start.27) | collective-permute-done | bytes 393248 | tf_op jit(solution)/shard_map/ppermute | solution.py:123
  124.9 3.2 %collective-permute-start.28 = (bf16[48,4096]{1,0:T(8,128)(2,1)S(1)}, bf16[48,4096]{1,0:T(8,128)(2,1)S(1)}, u32[]{:S(2)}, u32[]{:S(2)}) collective-permute-start(bf16[48,4096]{1,0:T(8,128)(2,1)S(1)} %add_convert_fusion), channel_id=1, source_target_pairs={{2,0},{15,1},{4,2},{1,3},{6,4},{3,5},{8,6},{5,7},{10,8},{7,9},{12,... | collective-permute-start | bytes 1179656 | tf_op jit(solution)/shard_map/ppermute | solution.py:128
  129.0 4.4 %collective-permute-done.28 = bf16[48,4096]{1,0:T(8,128)(2,1)S(1)} collective-permute-done((bf16[48,4096]{1,0:T(8,128)(2,1)S(1)}, bf16[48,4096]{1,0:T(8,128)(2,1)S(1)}, u32[]{:S(2)}, u32[]{:S(2)}) %collective-permute-start.28) | collective-permute-done | bytes 393248 | tf_op jit(solution)/shard_map/ppermute | solution.py:128
  133.9 1.0 collective-permute-done.29
  135.2 14.2 %all_to_all.10 = bf16[8,3,4096]{2,1,0:T(4,128)(2,1)S(1)} all-to-all(bf16[8,3,4096]{2,1,0:T(4,128)(2,1)S(1)} %reshape.56), channel_id=1, replica_groups=mesh['xh'=2,'y'=4,'xl'=2,'z'=8,'c'=2] {'xh','y'}, dimensions={0} | all-to-all | bytes 393216 | tf_op jit(solution)/shard_map/all_to_all | solution.py:158
  (94 shorter events, 17.2 us)
Async XLA Ops:
  2.5 17.2 %all-to-all-start = ((bf16[8,3,4096]{2,1,0:T(4,128)(2,1)}), bf16[8,3,4096]{2,1,0:T(4,128)(2,1)S(1)}, u32[]{:S(2)}, u32[]{:S(2)}) async-start(bf16[8,3,4096]{2,1,0:T(4,128)(2,1)} %reshape.54), calls=%async_computation | async-start | bytes 524288 | tf_op jit(solution)/shard_map/all_to_all | solution.py:154
  19.9 1.5 %collective-permute-start.4 = (bf16[24,4096]{1,0:T(8,128)(2,1)S(1)}, bf16[24,4096]{1,0:T(8,128)(2,1)S(1)}, u32[]{:S(2)}, u32[]{:S(2)}) collective-permute-start(bf16[24,4096]{1,0:T(8,128)(2,1)S(1)} %reshape.55), channel_id=1, source_target_pairs={{0,1},{1,0},{2,3},{3,2},{4,5},{5,4},{6,7},{7,6},{8,9},{9,8},{10,11... | collective-permute-start | bytes 589832 | tf_op jit(solution)/shard_map/ppermute | solution.py:105
  20.0 54.2 %copy-start.4 = (bf16[448,4096]{1,0:T(8,128)(2,1)S(1)}, bf16[448,4096]{1,0:T(8,128)(2,1)}, u32[]{:S(2)}) copy-start(bf16[448,4096]{1,0:T(8,128)(2,1)} %copy-done.3) | copy-start | bytes 11010052
  20.0 7.4 %collective-permute-start = (bf16[24,4096]{1,0:T(8,128)(2,1)S(1)}, bf16[24,4096]{1,0:T(8,128)(2,1)S(1)}, u32[]{:S(2)}, u32[]{:S(2)}) collective-permute-start(bf16[24,4096]{1,0:T(8,128)(2,1)S(1)} %reshape.55), channel_id=1, source_target_pairs={{0,16},{16,0},{1,17},{17,1},{2,18},{18,2},{3,19},{19,3},{4,20},{20... | collective-permute-start | bytes 589832 | tf_op jit(solution)/shard_map/ppermute | solution.py:114
  21.4 11.7 %collective-permute-start.5 = (bf16[48,4096]{1,0:T(8,128)(2,1)S(1)}, bf16[48,4096]{1,0:T(8,128)(2,1)S(1)}, u32[]{:S(2)}, u32[]{:S(2)}) collective-permute-start(bf16[48,4096]{1,0:T(8,128)(2,1)S(1)} %pad_maximum_fusion), channel_id=1, source_target_pairs={{0,2},{1,15},{2,4},{3,1},{4,6},{5,3},{6,8},{7,5},{8,10},{9,7},{10,... | collective-permute-start | bytes 1179656 | tf_op jit(solution)/shard_map/ppermute | solution.py:109
  27.4 91.5 %collective-permute-start.1 = (bf16[48,4096]{1,0:T(8,128)(2,1)S(1)}, bf16[48,4096]{1,0:T(8,128)(2,1)S(1)}, u32[]{:S(2)}, u32[]{:S(2)}) collective-permute-start(bf16[48,4096]{1,0:T(8,128)(2,1)S(1)} %constant_dynamic-update-slice_fusion.own_ref), channel_id=1, source_target_pairs={{0,1},{1,0},{2,3},{3,2},{4,5},{5,4},{6,7},{7,6},{8,9},{9,8},{10,11... | collective-permute-start | bytes 1179656 | tf_op jit(solution)/shard_map/ppermute | solution.py:115
  33.1 11.9 %collective-permute-start.10 = (bf16[48,4096]{1,0:T(8,128)(2,1)S(1)}, bf16[48,4096]{1,0:T(8,128)(2,1)S(1)}, u32[]{:S(2)}, u32[]{:S(2)}) collective-permute-start(bf16[48,4096]{1,0:T(8,128)(2,1)S(1)} %collective-permute-done.5), channel_id=1, source_target_pairs={{0,2},{1,15},{2,4},{3,1},{4,6},{5,3},{6,8},{7,5},{8,10},{9,7},{10,... | collective-permute-start | bytes 1179656 | tf_op jit(solution)/shard_map/ppermute | solution.py:109
  33.1 11.0 %collective-permute-start.6 = (bf16[48,4096]{1,0:T(8,128)(2,1)S(1)}, bf16[48,4096]{1,0:T(8,128)(2,1)S(1)}, u32[]{:S(2)}, u32[]{:S(2)}) collective-permute-start(bf16[48,4096]{1,0:T(8,128)(2,1)S(1)} %collective-permute-done.5), channel_id=1, source_target_pairs={{0,16},{16,0},{1,17},{17,1},{2,18},{18,2},{3,19},{19,3},{4,20},{20... | collective-permute-start | bytes 1179656 | tf_op jit(solution)/shard_map/ppermute | solution.py:114
  44.2 35.2 %collective-permute-start.7 = (bf16[96,4096]{1,0:T(8,128)(2,1)S(1)}, bf16[96,4096]{1,0:T(8,128)(2,1)S(1)}, u32[]{:S(2)}, u32[]{:S(2)}) collective-permute-start(bf16[96,4096]{1,0:T(8,128)(2,1)S(1)} %constant_dynamic-update-slice_fusion.2.own_ref), channel_id=1, source_target_pairs={{0,1},{1,0},{2,3},{3,2},{4,5},{5,4},{6,7},{7,6},{8,9},{9,8},{10,11... | collective-permute-start | bytes 2359304 | tf_op jit(solution)/shard_map/ppermute | solution.py:115
  45.1 9.0 %collective-permute-start.15 = (bf16[48,4096]{1,0:T(8,128)(2,1)S(1)}, bf16[48,4096]{1,0:T(8,128)(2,1)S(1)}, u32[]{:S(2)}, u32[]{:S(2)}) collective-permute-start(bf16[48,4096]{1,0:T(8,128)(2,1)S(1)} %collective-permute-done.10), channel_id=1, source_target_pairs={{0,2},{1,15},{2,4},{3,1},{4,6},{5,3},{6,8},{7,5},{8,10},{9,7},{10,... | collective-permute-start | bytes 1179656 | tf_op jit(solution)/shard_map/ppermute | solution.py:109
  45.1 11.3 %collective-permute-start.11 = (bf16[48,4096]{1,0:T(8,128)(2,1)S(1)}, bf16[48,4096]{1,0:T(8,128)(2,1)S(1)}, u32[]{:S(2)}, u32[]{:S(2)}) collective-permute-start(bf16[48,4096]{1,0:T(8,128)(2,1)S(1)} %collective-permute-done.10), channel_id=1, source_target_pairs={{0,16},{16,0},{1,17},{17,1},{2,18},{18,2},{3,19},{19,3},{4,20},{20... | collective-permute-start | bytes 1179656 | tf_op jit(solution)/shard_map/ppermute | solution.py:114
  54.1 7.0 %collective-permute-start.20 = (bf16[24,4096]{1,0:T(8,128)(2,1)S(1)}, bf16[24,4096]{1,0:T(8,128)(2,1)S(1)}, u32[]{:S(2)}, u32[]{:S(2)}) collective-permute-start(bf16[24,4096]{1,0:T(8,128)(2,1)S(1)} %slice.110), channel_id=1, source_target_pairs={{0,2},{1,15},{2,4},{3,1},{4,6},{5,3},{6,8},{7,5},{8,10},{9,7},{10,... | collective-permute-start | bytes 589832 | tf_op jit(solution)/shard_map/ppermute | solution.py:109
  56.4 26.6 %collective-permute-start.12 = (bf16[96,4096]{1,0:T(8,128)(2,1)S(1)}, bf16[96,4096]{1,0:T(8,128)(2,1)S(1)}, u32[]{:S(2)}, u32[]{:S(2)}) collective-permute-start(bf16[96,4096]{1,0:T(8,128)(2,1)S(1)} %constant_dynamic-update-slice_fusion.4.own_ref), channel_id=1, source_target_pairs={{0,1},{1,0},{2,3},{3,2},{4,5},{5,4},{6,7},{7,6},{8,9},{9,8},{10,11... | collective-permute-start | bytes 2359304 | tf_op jit(solution)/shard_map/ppermute | solution.py:115
  57.0 15.5 %collective-permute-start.16 = (bf16[48,4096]{1,0:T(8,128)(2,1)S(1)}, bf16[48,4096]{1,0:T(8,128)(2,1)S(1)}, u32[]{:S(2)}, u32[]{:S(2)}) collective-permute-start(bf16[48,4096]{1,0:T(8,128)(2,1)S(1)} %collective-permute-done.15), channel_id=1, source_target_pairs={{0,16},{16,0},{1,17},{17,1},{2,18},{18,2},{3,19},{19,3},{4,20},{20... | collective-permute-start | bytes 1179656 | tf_op jit(solution)/shard_map/ppermute | solution.py:114
  61.0 11.3 %collective-permute-start.21 = (bf16[24,4096]{1,0:T(8,128)(2,1)S(1)}, bf16[24,4096]{1,0:T(8,128)(2,1)S(1)}, u32[]{:S(2)}, u32[]{:S(2)}) collective-permute-start(bf16[24,4096]{1,0:T(8,128)(2,1)S(1)} %collective-permute-done.20), channel_id=1, source_target_pairs={{0,16},{16,0},{1,17},{17,1},{2,18},{18,2},{3,19},{19,3},{4,20},{20... | collective-permute-start | bytes 589832 | tf_op jit(solution)/shard_map/ppermute | solution.py:114
  72.4 1.8 %collective-permute-start.22 = (bf16[48,4096]{1,0:T(8,128)(2,1)S(1)}, bf16[48,4096]{1,0:T(8,128)(2,1)S(1)}, u32[]{:S(2)}, u32[]{:S(2)}) collective-permute-start(bf16[48,4096]{1,0:T(8,128)(2,1)S(1)} %constant_dynamic-update-slice_fusion.8.own_ref), channel_id=1, source_target_pairs={{0,1},{1,0},{2,3},{3,2},{4,5},{5,4},{6,7},{7,6},{8,9},{9,8},{10,11... | collective-permute-start | bytes 1179656 | tf_op jit(solution)/shard_map/ppermute | solution.py:115
  72.5 14.6 %collective-permute-start.17 = (bf16[96,4096]{1,0:T(8,128)(2,1)S(1)}, bf16[96,4096]{1,0:T(8,128)(2,1)S(1)}, u32[]{:S(2)}, u32[]{:S(2)}) collective-permute-start(bf16[96,4096]{1,0:T(8,128)(2,1)S(1)} %constant_dynamic-update-slice_fusion.6.own_ref), channel_id=1, source_target_pairs={{0,1},{1,0},{2,3},{3,2},{4,5},{5,4},{6,7},{7,6},{8,9},{9,8},{10,11... | collective-permute-start | bytes 2359304 | tf_op jit(solution)/shard_map/ppermute | solution.py:115
  79.2 7.1 %collective-permute-start.23 = (bf16[48,4096]{1,0:T(8,128)(2,1)S(1)}, bf16[48,4096]{1,0:T(8,128)(2,1)S(1)}, u32[]{:S(2)}, u32[]{:S(2)}) collective-permute-start(bf16[48,4096]{1,0:T(8,128)(2,1)S(1)} %get-tuple-element.30), channel_id=1, source_target_pairs={{0,1},{1,0},{2,3},{3,2},{4,5},{5,4},{6,7},{7,6},{8,9},{9,8},{10,11... | collective-permute-start | bytes 1179656 | tf_op jit(solution)/shard_map/ppermute | solution.py:117
  82.5 27.1 %collective-permute-start.8 = (bf16[96,4096]{1,0:T(8,128)(2,1)S(1)}, bf16[96,4096]{1,0:T(8,128)(2,1)S(1)}, u32[]{:S(2)}, u32[]{:S(2)}) collective-permute-start(bf16[96,4096]{1,0:T(8,128)(2,1)S(1)} %get-tuple-element.24), channel_id=1, source_target_pairs={{0,1},{1,0},{2,3},{3,2},{4,5},{5,4},{6,7},{7,6},{8,9},{9,8},{10,11... | collective-permute-start | bytes 2359304 | tf_op jit(solution)/shard_map/ppermute | solution.py:117
  86.1 11.0 %collective-permute-start.13 = (bf16[96,4096]{1,0:T(8,128)(2,1)S(1)}, bf16[96,4096]{1,0:T(8,128)(2,1)S(1)}, u32[]{:S(2)}, u32[]{:S(2)}) collective-permute-start(bf16[96,4096]{1,0:T(8,128)(2,1)S(1)} %get-tuple-element.26), channel_id=1, source_target_pairs={{0,1},{1,0},{2,3},{3,2},{4,5},{5,4},{6,7},{7,6},{8,9},{9,8},{10,11... | collective-permute-start | bytes 2359304 | tf_op jit(solution)/shard_map/ppermute | solution.py:117
  86.4 7.3 %collective-permute-start.24 = (bf16[24,4096]{1,0:T(8,128)(2,1)S(1)}, bf16[24,4096]{1,0:T(8,128)(2,1)S(1)}, u32[]{:S(2)}, u32[]{:S(2)}) collective-permute-start(bf16[24,4096]{1,0:T(8,128)(2,1)S(1)} %add_convert_fusion.7), channel_id=1, source_target_pairs={{0,16},{16,0},{1,17},{17,1},{2,18},{18,2},{3,19},{19,3},{4,20},{20... | collective-permute-start | bytes 589832 | tf_op jit(solution)/shard_map/ppermute | solution.py:119
  90.3 5.9 %collective-permute-start.18 = (bf16[96,4096]{1,0:T(8,128)(2,1)S(1)}, bf16[96,4096]{1,0:T(8,128)(2,1)S(1)}, u32[]{:S(2)}, u32[]{:S(2)}) collective-permute-start(bf16[96,4096]{1,0:T(8,128)(2,1)S(1)} %get-tuple-element.28), channel_id=1, source_target_pairs={{0,1},{1,0},{2,3},{3,2},{4,5},{5,4},{6,7},{7,6},{8,9},{9,8},{10,11... | collective-permute-start | bytes 2359304 | tf_op jit(solution)/shard_map/ppermute | solution.py:117
  93.7 14.7 %collective-permute-start.25 = (bf16[24,4096]{1,0:T(8,128)(2,1)S(1)}, bf16[24,4096]{1,0:T(8,128)(2,1)S(1)}, u32[]{:S(2)}, u32[]{:S(2)}) collective-permute-start(bf16[24,4096]{1,0:T(8,128)(2,1)S(1)} %add_convert_fusion.6), channel_id=1, source_target_pairs={{2,0},{15,1},{4,2},{1,3},{6,4},{3,5},{8,6},{5,7},{10,8},{7,9},{12,... | collective-permute-start | bytes 589832 | tf_op jit(solution)/shard_map/ppermute | solution.py:123
  96.2 12.1 %collective-permute-start.19 = (bf16[48,4096]{1,0:T(8,128)(2,1)S(1)}, bf16[48,4096]{1,0:T(8,128)(2,1)S(1)}, u32[]{:S(2)}, u32[]{:S(2)}) collective-permute-start(bf16[48,4096]{1,0:T(8,128)(2,1)S(1)} %add_convert_fusion.2), channel_id=1, source_target_pairs={{0,16},{16,0},{1,17},{17,1},{2,18},{18,2},{3,19},{19,3},{4,20},{20... | collective-permute-start | bytes 1179656 | tf_op jit(solution)/shard_map/ppermute | solution.py:119
  97.2 19.5 %collective-permute-start.14 = (bf16[48,4096]{1,0:T(8,128)(2,1)S(1)}, bf16[48,4096]{1,0:T(8,128)(2,1)S(1)}, u32[]{:S(2)}, u32[]{:S(2)}) collective-permute-start(bf16[48,4096]{1,0:T(8,128)(2,1)S(1)} %add_convert_fusion.3), channel_id=1, source_target_pairs={{0,16},{16,0},{1,17},{17,1},{2,18},{18,2},{3,19},{19,3},{4,20},{20... | collective-permute-start | bytes 1179656 | tf_op jit(solution)/shard_map/ppermute | solution.py:119
  108.5 8.2 %collective-permute-start.26 = (bf16[48,4096]{1,0:T(8,128)(2,1)S(1)}, bf16[48,4096]{1,0:T(8,128)(2,1)S(1)}, u32[]{:S(2)}, u32[]{:S(2)}) collective-permute-start(bf16[48,4096]{1,0:T(8,128)(2,1)S(1)} %pad_maximum_fusion.1), channel_id=1, source_target_pairs={{2,0},{15,1},{4,2},{1,3},{6,4},{3,5},{8,6},{5,7},{10,8},{7,9},{12,... | collective-permute-start | bytes 1179656 | tf_op jit(solution)/shard_map/ppermute | solution.py:123
  109.7 12.2 %collective-permute-start.9 = (bf16[48,4096]{1,0:T(8,128)(2,1)S(1)}, bf16[48,4096]{1,0:T(8,128)(2,1)S(1)}, u32[]{:S(2)}, u32[]{:S(2)}) collective-permute-start(bf16[48,4096]{1,0:T(8,128)(2,1)S(1)} %add_convert_fusion.4), channel_id=1, source_target_pairs={{0,16},{16,0},{1,17},{17,1},{2,18},{18,2},{3,19},{19,3},{4,20},{20... | collective-permute-start | bytes 1179656 | tf_op jit(solution)/shard_map/ppermute | solution.py:119
  116.9 7.9 %collective-permute-start.27 = (bf16[48,4096]{1,0:T(8,128)(2,1)S(1)}, bf16[48,4096]{1,0:T(8,128)(2,1)S(1)}, u32[]{:S(2)}, u32[]{:S(2)}) collective-permute-start(bf16[48,4096]{1,0:T(8,128)(2,1)S(1)} %add_convert_fusion.1), channel_id=1, source_target_pairs={{2,0},{15,1},{4,2},{1,3},{6,4},{3,5},{8,6},{5,7},{10,8},{7,9},{12,... | collective-permute-start | bytes 1179656 | tf_op jit(solution)/shard_map/ppermute | solution.py:123
  121.8 6.3 %collective-permute-start.2 = (bf16[48,4096]{1,0:T(8,128)(2,1)S(1)}, bf16[48,4096]{1,0:T(8,128)(2,1)S(1)}, u32[]{:S(2)}, u32[]{:S(2)}) collective-permute-start(bf16[48,4096]{1,0:T(8,128)(2,1)S(1)} %get-tuple-element.22), channel_id=1, source_target_pairs={{0,1},{1,0},{2,3},{3,2},{4,5},{5,4},{6,7},{7,6},{8,9},{9,8},{10,11... | collective-permute-start | bytes 1179656 | tf_op jit(solution)/shard_map/ppermute | solution.py:117
  124.9 8.5 %collective-permute-start.28 = (bf16[48,4096]{1,0:T(8,128)(2,1)S(1)}, bf16[48,4096]{1,0:T(8,128)(2,1)S(1)}, u32[]{:S(2)}, u32[]{:S(2)}) collective-permute-start(bf16[48,4096]{1,0:T(8,128)(2,1)S(1)} %add_convert_fusion), channel_id=1, source_target_pairs={{2,0},{15,1},{4,2},{1,3},{6,4},{3,5},{8,6},{5,7},{10,8},{7,9},{12,... | collective-permute-start | bytes 1179656 | tf_op jit(solution)/shard_map/ppermute | solution.py:128
  128.2 5.8 %collective-permute-start.3 = (bf16[24,4096]{1,0:T(8,128)(2,1)S(1)}, bf16[24,4096]{1,0:T(8,128)(2,1)S(1)}, u32[]{:S(2)}, u32[]{:S(2)}) collective-permute-start(bf16[24,4096]{1,0:T(8,128)(2,1)S(1)} %add_convert_fusion.8), channel_id=1, source_target_pairs={{0,16},{16,0},{1,17},{17,1},{2,18},{18,2},{3,19},{19,3},{4,20},{20... | collective-permute-start | bytes 589832 | tf_op jit(solution)/shard_map/ppermute | solution.py:119
  133.4 1.5 %collective-permute-start.29 = (bf16[24,4096]{1,0:T(8,128)(2,1)S(1)}, bf16[24,4096]{1,0:T(8,128)(2,1)S(1)}, u32[]{:S(2)}, u32[]{:S(2)}) collective-permute-start(bf16[24,4096]{1,0:T(8,128)(2,1)S(1)} %slice.115), channel_id=1, source_target_pairs={{0,1},{1,0},{2,3},{3,2},{4,5},{5,4},{6,7},{7,6},{8,9},{9,8},{10,11... | collective-permute-start | bytes 589832 | tf_op jit(solution)/shard_map/ppermute | solution.py:129
  (7 other events, 58.8 us)
